TPU v7x, 32 devices: a whole 2x2x4 slice. The times are simulated.
32 devices in a mesh: seq: 8 (over z, core), fsdp: 4 (over y, x).
Axes of the slice: x: 2, y: 2, z: 4, core: 2. Of those that a mesh axis runs over, the one named last changes fastest.
Arguments:
- tokens: bfloat16 [4, 4, 1024, 768], P(None, 'fsdp', 'seq'), may hold values from -6 to 6
- segments: int32 [4, 4, 1024], P(None, 'fsdp', 'seq'), may hold values from 0 to 3, never falling along the last dimension, each value on 1 to 512 neighbouring positions
- w_query: bfloat16 [768, 768], P('fsdp'), may hold values from -0.4375 to 0.4375
- w_key: bfloat16 [768, 768], P('fsdp'), may hold values from -0.21875 to 0.21875
- w_value: bfloat16 [768, 768], P('fsdp'), may hold values from -0.21875 to 0.21875
- w_out: bfloat16 [768, 768], P('fsdp'), may hold values from -0.625 to 0.625
- w_gate: bfloat16 [768, 2048], P('fsdp'), may hold values from -0.21875 to 0.21875
- w_up: bfloat16 [768, 2048], P('fsdp'), may hold values from -0.21875 to 0.21875
- w_down: bfloat16 [2048, 768], P('fsdp'), may hold values from -0.125 to 0.125
- gain_attn: bfloat16 [768], P('fsdp'), may hold values from 0.099609375 to 1.8984375
- gain_ffn: bfloat16 [768], P('fsdp'), may hold values from 0.099609375 to 1.8984375
- cotangent: bfloat16 [4, 4, 1024, 768], P(None, 'fsdp', 'seq'), may hold values from -6 to 6
Outputs:
- output: bfloat16 [4, 4, 1024, 768], P(None, 'fsdp', 'seq')
- input_grad: bfloat16 [4, 4, 1024, 768], P(None, 'fsdp', 'seq')
- w_query_grad: float32 [768, 768], P('fsdp')
- w_key_grad: float32 [768, 768], P('fsdp')
- w_value_grad: float32 [768, 768], P('fsdp')
- w_out_grad: float32 [768, 768], P('fsdp')
- w_gate_grad: float32 [768, 2048], P('fsdp')
- w_up_grad: float32 [768, 2048], P('fsdp')
- w_down_grad: float32 [2048, 768], P('fsdp')
- gain_attn_grad: float32 [768], P('fsdp')
- gain_ffn_grad: float32 [768], P('fsdp')
Inputs may be any that keep to these rules, and one draw needn't show every extreme that they name: `segments`: along each sequence the document number never falls; every document of 0 to 3 holds 1 to 512 tokens, and one holds exactly 512.
All inputs are finite; a program needn't handle non-finite values.
Results may differ from a plain program's by a relative error of at most 0.024.
Values may be sent and summed in bfloat16 or wider, within the bound.
No kernel may reach another device: no remote copies, remote signals or barrier semaphores. Data moves between devices by JAX's collectives and lax.ppermute only.
A program may use at most 192 MiB of HBM per device.

v0:
```python
import math

import jax
import jax.numpy as jnp
from jax import lax
from jax.sharding import PartitionSpec as P

HEADS = 12
DOCS = 4


EPS = 1e-06
NEGATIVE = -1e30


def for_sending(value):

    def short(part):
        return part.astype(jnp.bfloat16) if part.dtype == jnp.float32 else part

    return jax.tree.map(short, value)


def angles(positions, head_size):
    half_size = head_size // 2
    frequency = 10000.0 ** (-jnp.arange(half_size, dtype=jnp.float32) / half_size)
    angle_rows = positions.astype(jnp.float32)[:, None] * frequency[None, :]
    angle_rows = jnp.concatenate([angle_rows, angle_rows], axis=-1)
    return (jnp.cos(angle_rows)[:, None, :], jnp.sin(angle_rows)[:, None, :])


def rotate(field_rows, cosine_rows, sine_rows):
    half_size = field_rows.shape[-1] // 2
    turned = jnp.concatenate([-field_rows[..., half_size:], field_rows[..., :half_size]], axis=-1)
    return field_rows * cosine_rows + turned * sine_rows


def rotate_back(gradient, cosine_rows, sine_rows):
    half_size = gradient.shape[-1] // 2
    sine_part = gradient * sine_rows
    return gradient * cosine_rows + jnp.concatenate(
        [sine_part[..., half_size:], -sine_part[..., :half_size]], axis=-1
    )


def normalize(value_rows, gain_vector):
    factor = lax.rsqrt(jnp.mean(value_rows * value_rows, axis=-1, keepdims=True) + EPS)
    unit_rows = value_rows * factor
    return (unit_rows * gain_vector, unit_rows, factor)


def normalize_back(gradient, unit_rows, factor, gain_vector):
    scaled_grad = gradient * gain_vector
    inner_mean = jnp.mean(scaled_grad * unit_rows, axis=-1, keepdims=True)
    return (factor * (scaled_grad - unit_rows * inner_mean), jnp.sum(gradient * unit_rows, axis=0))


def masked_scores(query_rows, key_rows, query_index, query_start, key_index, score_scale):
    scores = (
        jnp.einsum("qhd,khd->hqk", query_rows, key_rows, preferred_element_type=jnp.float32)
        * score_scale
    )
    visible = (key_index[None, :] <= query_index[:, None]) & (
        key_index[None, :] >= query_start[:, None]
    )
    return (scores, visible[None])


def block_live(first_row, block_rows, lowest, highest):
    return (first_row <= highest) & (first_row + block_rows - 1 >= lowest)


def attend(query_rows, key_blocks, value_blocks, query_index, query_start, score_scale):
    block_count, block_rows, head_count, head_size = key_blocks.shape
    query_count = query_rows.shape[0]
    lowest = jnp.min(query_start)
    highest = jnp.max(query_index)
    numbers = jnp.arange(block_count, dtype=jnp.int32)

    def stat_step(carry_state, block_item):
        number, key_rows = block_item
        key_index = number * block_rows + jnp.arange(block_rows, dtype=jnp.int32)

        def stat_compute(running):
            running_max, running_sum = running
            scores, visible = masked_scores(
                query_rows, key_rows, query_index, query_start, key_index, score_scale
            )
            new_max = jnp.maximum(
                running_max, jnp.max(jnp.where(visible, scores, NEGATIVE), axis=-1)
            )
            block_sum = jnp.sum(
                jnp.where(visible, jnp.exp(scores - new_max[:, :, None]), 0.0), axis=-1
            )
            return (new_max, running_sum * jnp.exp(running_max - new_max) + block_sum)

        is_live = block_live(number * block_rows, block_rows, lowest, highest)
        return (lax.cond(is_live, stat_compute, lambda running: running, carry_state), None)

    start_state = (
        jnp.full((head_count, query_count), NEGATIVE, jnp.float32),
        jnp.zeros((head_count, query_count), jnp.float32),
    )
    (final_max, final_sum), _ = lax.scan(stat_step, start_state, (numbers, key_blocks))
    log_total = final_max + jnp.log(final_sum)

    def out_step(accumulated, block_item):
        number, key_rows, value_rows = block_item
        key_index = number * block_rows + jnp.arange(block_rows, dtype=jnp.int32)

        def out_compute(running):
            scores, visible = masked_scores(
                query_rows, key_rows, query_index, query_start, key_index, score_scale
            )
            weight_rows = jnp.where(visible, jnp.exp(scores - log_total[:, :, None]), 0.0)
            return running + jnp.einsum(
                "hqk,khd->qhd",
                weight_rows.astype(jnp.bfloat16),
                value_rows,
                preferred_element_type=jnp.float32,
            )

        is_live = block_live(number * block_rows, block_rows, lowest, highest)
        return (lax.cond(is_live, out_compute, lambda running: running, accumulated), None)

    attended, _ = lax.scan(
        out_step,
        jnp.zeros((query_count, head_count, head_size), jnp.float32),
        (numbers, key_blocks, value_blocks),
    )
    return (attended, log_total)


def pair_grads(
    query_rows,
    grad_rows,
    log_total,
    row_dots,
    key_rows,
    value_rows,
    query_index,
    query_start,
    key_index,
    score_scale,
):
    scores, visible = masked_scores(
        query_rows, key_rows, query_index, query_start, key_index, score_scale
    )
    weight_rows = jnp.where(visible, jnp.exp(scores - log_total[:, :, None]), 0.0)
    value_part = jnp.einsum(
        "hqk,qhd->khd",
        weight_rows.astype(jnp.bfloat16),
        grad_rows,
        preferred_element_type=jnp.float32,
    )
    prob_grad = jnp.einsum(
        "qhd,khd->hqk", grad_rows, value_rows, preferred_element_type=jnp.float32
    )
    score_grad = (weight_rows * (prob_grad - row_dots[:, :, None])).astype(jnp.bfloat16)
    query_part = (
        jnp.einsum("hqk,khd->qhd", score_grad, key_rows, preferred_element_type=jnp.float32)
        * score_scale
    )
    key_part = (
        jnp.einsum("hqk,qhd->khd", score_grad, query_rows, preferred_element_type=jnp.float32)
        * score_scale
    )
    return (query_part, key_part, value_part)


def body(
    tokens,
    segments,
    w_query,
    w_key,
    w_value,
    w_out,
    w_gate,
    w_up,
    w_down,
    gain_attn,
    gain_ffn,
    cotangent,
):
    micro_count = tokens.shape[0]
    span_rows = tokens.shape[2]
    model_width = tokens.shape[3]
    head_count = HEADS
    head_size = model_width // head_count
    score_scale = 1.0 / math.sqrt(head_size)
    cycle_size = lax.axis_size("seq")
    seq_tokens = span_rows * cycle_size
    group_size = 1
    while group_size * 2 * span_rows <= 512 and cycle_size % (group_size * 2) == 0:
        group_size = group_size * 2
    block_rows = group_size * span_rows
    block_count = cycle_size // group_size
    numbers = jnp.arange(block_count, dtype=jnp.int32)
    first_key = lax.axis_index("seq") * span_rows
    doc_ids = jnp.arange(DOCS, dtype=jnp.int32)
    membership = (segments[:, 0, :, None] == doc_ids).astype(jnp.int32)
    doc_totals = lax.psum(jnp.sum(membership, axis=1), "seq")
    before = jnp.cumsum(doc_totals, axis=1) - doc_totals
    starts = jnp.sum(membership * before[:, None, :], axis=2)
    positions = first_key + jnp.arange(span_rows, dtype=jnp.int32)
    summed = None
    outputs = []
    input_grads = []
    for index_micro in range(micro_count):
        gathered = (
            lax.all_gather(w_query, "fsdp", axis=0, tiled=True),
            lax.all_gather(w_key, "fsdp", axis=0, tiled=True),
            lax.all_gather(w_value, "fsdp", axis=0, tiled=True),
            lax.all_gather(w_out, "fsdp", axis=0, tiled=True),
            lax.all_gather(w_gate, "fsdp", axis=0, tiled=True),
            lax.all_gather(w_up, "fsdp", axis=0, tiled=True),
            lax.all_gather(w_down, "fsdp", axis=0, tiled=True),
            lax.all_gather(gain_attn, "fsdp", axis=0, tiled=True),
            lax.all_gather(gain_ffn, "fsdp", axis=0, tiled=True),
        )
        (
            full_query,
            full_key,
            full_value,
            full_out,
            full_gate,
            full_up,
            full_down,
            full_gain_attn,
            full_gain_ffn,
        ) = gathered
        gain_one = full_gain_attn.astype(jnp.float32)
        gain_two = full_gain_ffn.astype(jnp.float32)
        hidden_in = tokens[index_micro, 0]
        query_start = starts[index_micro]
        cosine_rows, sine_rows = angles(positions - query_start, head_size)
        query_lin = jnp.dot(hidden_in, full_query, preferred_element_type=jnp.float32).reshape(
            span_rows, head_count, head_size
        )
        key_lin = jnp.dot(hidden_in, full_key, preferred_element_type=jnp.float32).reshape(
            span_rows, head_count, head_size
        )
        queries = rotate(query_lin, cosine_rows, sine_rows).astype(jnp.bfloat16)
        keys_own = rotate(key_lin, cosine_rows, sine_rows).astype(jnp.bfloat16)
        values_own = jnp.dot(hidden_in, full_value, preferred_element_type=jnp.float32).astype(
            jnp.bfloat16
        )
        keys_all, values_all = (
            lax.all_gather(keys_own.reshape(span_rows, model_width), "seq", axis=0, tiled=True),
            lax.all_gather(values_own, "seq", axis=0, tiled=True),
        )
        key_blocks = keys_all.reshape(block_count, block_rows, head_count, head_size)
        value_blocks = values_all.reshape(block_count, block_rows, head_count, head_size)
        attended, log_total = attend(
            queries, key_blocks, value_blocks, positions, query_start, score_scale
        )
        attended_low = attended.reshape(span_rows, model_width).astype(jnp.bfloat16)
        branch = jnp.dot(attended_low, full_out, preferred_element_type=jnp.float32)
        middle, unit_one, factor_one = normalize(hidden_in.astype(jnp.float32) + branch, gain_one)
        middle_low = middle.astype(jnp.bfloat16)
        gate_pre = jnp.dot(middle_low, full_gate, preferred_element_type=jnp.float32)
        up_pre = jnp.dot(middle_low, full_up, preferred_element_type=jnp.float32)
        gate_sig = jax.nn.sigmoid(gate_pre)
        gate_silu = gate_pre * gate_sig
        hidden_low = (gate_silu * up_pre).astype(jnp.bfloat16)
        ffn_out = jnp.dot(hidden_low, full_down, preferred_element_type=jnp.float32)
        result, unit_two, factor_two = normalize(middle + ffn_out, gain_two)
        outputs.append(result.astype(jnp.bfloat16))
        cot_rows = cotangent[index_micro, 0].astype(jnp.float32)
        ffn_grad, gain_ffn_grad = normalize_back(cot_rows, unit_two, factor_two, gain_two)
        ffn_grad_low = ffn_grad.astype(jnp.bfloat16)
        down_w_grad = jnp.einsum(
            "cf,cd->fd", hidden_low, ffn_grad_low, preferred_element_type=jnp.float32
        )
        hidden_grad = jnp.einsum(
            "cd,fd->cf", ffn_grad_low, full_down, preferred_element_type=jnp.float32
        )
        gate_grad_low = (
            hidden_grad * up_pre * gate_sig * (1.0 + gate_pre * (1.0 - gate_sig))
        ).astype(jnp.bfloat16)
        up_grad_low = (hidden_grad * gate_silu).astype(jnp.bfloat16)
        gate_w_grad = jnp.einsum(
            "cd,cf->df", middle_low, gate_grad_low, preferred_element_type=jnp.float32
        )
        up_w_grad = jnp.einsum(
            "cd,cf->df", middle_low, up_grad_low, preferred_element_type=jnp.float32
        )
        middle_grad = (
            ffn_grad
            + jnp.einsum("cf,df->cd", gate_grad_low, full_gate, preferred_element_type=jnp.float32)
            + jnp.einsum("cf,df->cd", up_grad_low, full_up, preferred_element_type=jnp.float32)
        )
        branch_grad, gain_attn_grad = normalize_back(middle_grad, unit_one, factor_one, gain_one)
        branch_grad_low = branch_grad.astype(jnp.bfloat16)
        out_w_grad = jnp.einsum(
            "cd,ce->de", attended_low, branch_grad_low, preferred_element_type=jnp.float32
        )
        attended_grad = (
            jnp.einsum("ce,de->cd", branch_grad_low, full_out, preferred_element_type=jnp.float32)
            .astype(jnp.bfloat16)
            .reshape(span_rows, head_count, head_size)
        )
        row_dots = jnp.sum(attended_grad.astype(jnp.float32) * attended, axis=-1).T
        lowest = jnp.min(query_start)
        highest = positions[span_rows - 1]

        def key_step(query_acc, block_item):
            number, key_rows, value_rows = block_item
            key_index = number * block_rows + jnp.arange(block_rows, dtype=jnp.int32)

            def key_compute(running):
                query_part, key_part, value_part = pair_grads(
                    queries,
                    attended_grad,
                    log_total,
                    row_dots,
                    key_rows,
                    value_rows,
                    positions,
                    query_start,
                    key_index,
                    score_scale,
                )
                return (running + query_part, (key_part, value_part))

            def skipped(running):
                zero_rows = jnp.zeros((block_rows, head_count, head_size), jnp.float32)
                return (running, (zero_rows, zero_rows))

            is_live = block_live(number * block_rows, block_rows, lowest, highest)
            return lax.cond(is_live, key_compute, skipped, query_acc)

        query_grad, (key_parts, value_parts) = lax.scan(
            key_step,
            jnp.zeros((span_rows, head_count, head_size), jnp.float32),
            (numbers, key_blocks, value_blocks),
        )
        key_grad, value_grad = (
            lax.psum_scatter(
                key_parts.reshape(seq_tokens, model_width).astype(jnp.bfloat16),
                "seq",
                scatter_dimension=0,
                tiled=True,
            ).astype(jnp.float32),
            lax.psum_scatter(
                value_parts.reshape(seq_tokens, model_width).astype(jnp.bfloat16),
                "seq",
                scatter_dimension=0,
                tiled=True,
            ).astype(jnp.float32),
        )
        key_grad = key_grad.reshape(span_rows, head_count, head_size)
        query_lin_grad = (
            rotate_back(query_grad, cosine_rows, sine_rows)
            .reshape(span_rows, model_width)
            .astype(jnp.bfloat16)
        )
        key_lin_grad = (
            rotate_back(key_grad, cosine_rows, sine_rows)
            .reshape(span_rows, model_width)
            .astype(jnp.bfloat16)
        )
        value_lin_grad = value_grad.astype(jnp.bfloat16)
        query_w_grad = jnp.einsum(
            "cd,ce->de", hidden_in, query_lin_grad, preferred_element_type=jnp.float32
        )
        key_w_grad = jnp.einsum(
            "cd,ce->de", hidden_in, key_lin_grad, preferred_element_type=jnp.float32
        )
        value_w_grad = jnp.einsum(
            "cd,ce->de", hidden_in, value_lin_grad, preferred_element_type=jnp.float32
        )
        input_grad = (
            branch_grad
            + jnp.einsum(
                "ce,de->cd", query_lin_grad, full_query, preferred_element_type=jnp.float32
            )
            + jnp.einsum("ce,de->cd", key_lin_grad, full_key, preferred_element_type=jnp.float32)
            + jnp.einsum(
                "ce,de->cd", value_lin_grad, full_value, preferred_element_type=jnp.float32
            )
        )
        input_grads.append(input_grad.astype(jnp.bfloat16))
        local_terms = (
            query_w_grad,
            key_w_grad,
            value_w_grad,
            out_w_grad,
            gate_w_grad,
            up_w_grad,
            down_w_grad,
            gain_attn_grad,
            gain_ffn_grad,
        )
        if summed is None:
            summed = local_terms
        else:
            summed = tuple((earlier + current for earlier, current in zip(summed, local_terms)))
    owned_sums = jax.tree.map(
        lambda part: part.astype(jnp.float32),
        lax.psum_scatter(for_sending(summed), "fsdp", scatter_dimension=0, tiled=True),
    )
    summed = jax.tree.map(
        lambda part: part.astype(jnp.float32), lax.psum(for_sending(owned_sums), "seq")
    )
    output = jnp.stack(outputs)[:, None]
    input_grad_all = jnp.stack(input_grads)[:, None]
    return (output, input_grad_all) + tuple(summed)


def solution(mesh):
    in_specs = (
        P(None, "fsdp", "seq", None),
        P(None, "fsdp", "seq"),
        P("fsdp", None),
        P("fsdp", None),
        P("fsdp", None),
        P("fsdp", None),
        P("fsdp", None),
        P("fsdp", None),
        P("fsdp", None),
        P("fsdp"),
        P("fsdp"),
        P(None, "fsdp", "seq", None),
    )
    out_specs = (
        P(None, "fsdp", "seq", None),
        P(None, "fsdp", "seq", None),
        P("fsdp", None),
        P("fsdp", None),
        P("fsdp", None),
        P("fsdp", None),
        P("fsdp", None),
        P("fsdp", None),
        P("fsdp", None),
        P("fsdp"),
        P("fsdp"),
    )
    return jax.shard_map(body, mesh=mesh, in_specs=in_specs, out_specs=out_specs, check_vma=False)
```

profile of v0, /device:TPU:0, one launch (start us, length us, event | category | flops | bytes accessed | tf_op | source)
XLA Modules:
  0.0 1210.2 jit_solution(12253551099931335162)
XLA Ops:
  10.3 10.6 psum.70
  22.6 17.7 %all-gather.20.cloned.1.call-done = bf16[768,768]{1,0:T(8,128)(2,1)} async-done(((bf16[192,768]{1,0:T(8,128)(2,1)}), bf16[768,768]{1,0:T(8,128)(2,1)}) %all-gather.20.cloned.1.call-update) | async-done | bytes 1179664 | tf_op jit(solution)/shard_map/all_gather | solution.py:211
  42.0 27.9 %all-gather.16.cloned.1.call-done = bf16[768,768]{1,0:T(8,128)(2,1)} async-done(((bf16[192,768]{1,0:T(8,128)(2,1)}), bf16[768,768]{1,0:T(8,128)(2,1)}) %all-gather.16.cloned.1.call-update) | async-done | bytes 1179664 | tf_op jit(solution)/shard_map/all_gather | solution.py:212
  75.5 24.0 %all-gather.22.cloned.1.call-done = bf16[768,768]{1,0:T(8,128)(2,1)} async-done(((bf16[192,768]{1,0:T(8,128)(2,1)}), bf16[768,768]{1,0:T(8,128)(2,1)}) %all-gather.22.cloned.1.call-update) | async-done | bytes 1179664 | tf_op jit(solution)/shard_map/all_gather | solution.py:213
  122.7 9.4 all-reduce.7
  134.1 3.9 reshape.1215
  139.6 15.4 %all-gather.24.cloned.1.call-done = bf16[1024,768]{1,0:T(8,128)(2,1)} async-done(((bf16[128,768]{1,0:T(8,128)(2,1)}), bf16[1024,768]{1,0:T(8,128)(2,1)}) %all-gather.24.cloned.1.call-update) | async-done | bytes 1572880 | tf_op jit(solution)/shard_map/all_gather | solution.py:250
  164.4 6.6 while.228
  171.0 7.4 while.229
  179.3 4.5 all-gather.34.cloned.1.call-done
  189.4 20.9 %all-gather.36.cloned.1.call-done = bf16[1024,768]{1,0:T(8,128)(2,1)} async-done(((bf16[128,768]{1,0:T(8,128)(2,1)}), bf16[1024,768]{1,0:T(8,128)(2,1)}) %all-gather.36.cloned.1.call-update) | async-done | bytes 1572880 | tf_op jit(solution)/shard_map/all_gather | solution.py:250
  217.2 6.6 while.230
  223.9 7.4 while.231
  232.1 7.0 all-gather.38.cloned.1.call-done
  244.7 20.9 %all-gather.40.cloned.1.call-done = bf16[1024,768]{1,0:T(8,128)(2,1)} async-done(((bf16[128,768]{1,0:T(8,128)(2,1)}), bf16[1024,768]{1,0:T(8,128)(2,1)}) %all-gather.40.cloned.1.call-update) | async-done | bytes 1572880 | tf_op jit(solution)/shard_map/all_gather | solution.py:250
  272.6 6.7 while.232
  279.4 7.4 while.233
  287.6 6.3 all-gather.42.cloned.1.call-done
  299.5 20.2 %all-gather.44.cloned.1.call-done = bf16[1024,768]{1,0:T(8,128)(2,1)} async-done(((bf16[128,768]{1,0:T(8,128)(2,1)}), bf16[1024,768]{1,0:T(8,128)(2,1)}) %all-gather.44.cloned.1.call-update) | async-done | bytes 1572880 | tf_op jit(solution)/shard_map/all_gather | solution.py:250
  326.7 6.8 while.234
  334.1 7.8 while.235
  342.7 6.0 all-gather.26.cloned.1.call-done
  353.1 41.4 %all-gather.28.cloned.1.call-done = bf16[768,2048]{1,0:T(8,128)(2,1)} async-done(((bf16[192,2048]{1,0:T(8,128)(2,1)}), bf16[768,2048]{1,0:T(8,128)(2,1)}) %all-gather.28.cloned.1.call-update) | async-done | bytes 3145744 | tf_op jit(solution)/shard_map/all_gather | solution.py:215
  397.0 43.2 %all-gather.30.cloned.1.call-done = bf16[768,2048]{1,0:T(8,128)(2,1)} async-done(((bf16[192,2048]{1,0:T(8,128)(2,1)}), bf16[768,2048]{1,0:T(8,128)(2,1)}) %all-gather.30.cloned.1.call-update) | async-done | bytes 3145744 | tf_op jit(solution)/shard_map/all_gather | solution.py:216
  443.9 42.0 %all-gather.32.cloned.1.call-done = bf16[2048,768]{1,0:T(8,128)(2,1)} async-done(((bf16[512,768]{1,0:T(8,128)(2,1)}), bf16[2048,768]{1,0:T(8,128)(2,1)}) %all-gather.32.cloned.1.call-update) | async-done | bytes 3145744 | tf_op jit(solution)/shard_map/all_gather | solution.py:217
  527.6 15.4 %while.239 = (s32[]{:T(128)}, f32[128,12,64]{0,2,1:T(8,128)}, bf16[2,512,12,64]{1,3,2,0:T(8,128)(2,1)}, bf16[2,512,12,64]{1,3,2,0:T(8,128)(2,1)}, s32[2]{0:T(128...) while((s32[]{:T(128)}, f32[128,12,64]{0,2,1:T(8,128)}, ...), condition=%wide.region_90.91_spmd.clone, body=%wide.region_87.90_spmd.clone.sunk | while | flops 512361088 | bytes 32497256 | solution.py:333
  530.9 6.6 conditional.47
  554.0 14.9 %while.238 = (s32[]{:T(128)}, f32[128,12,64]{0,2,1:T(8,128)}, bf16[2,512,12,64]{1,3,2,0:T(8,128)(2,1)}, bf16[2,512,12,64]{1,3,2,0:T(8,128)(2,1)}, s32[2]{0:T(128...) while((s32[]{:T(128)}, f32[128,12,64]{0,2,1:T(8,128)}, ...), condition=%wide.region_81.82_spmd.clone, body=%wide.region_78.81_spmd.clone.sunk | while | flops 512361088 | bytes 32474580 | solution.py:333
  556.8 6.6 conditional.46
  578.6 13.1 %while.237 = (s32[]{:T(128)}, f32[128,12,64]{0,2,1:T(8,128)}, bf16[2,512,12,64]{1,3,2,0:T(8,128)(2,1)}, bf16[2,512,12,64]{1,3,2,0:T(8,128)(2,1)}, s32[2]{0:T(128...) while((s32[]{:T(128)}, f32[128,12,64]{0,2,1:T(8,128)}, ...), condition=%wide.region_72.73_spmd.clone, body=%wide.region_69.72_spmd.clone.sunk | while | flops 512361088 | bytes 32499304 | solution.py:333
  581.5 4.7 conditional.45
  601.3 13.1 %while.236 = (s32[]{:T(128)}, f32[128,12,64]{0,2,1:T(8,128)}, bf16[2,512,12,64]{1,3,2,0:T(8,128)(2,1)}, bf16[2,512,12,64]{1,3,2,0:T(8,128)(2,1)}, s32[2]{0:T(128...) while((s32[]{:T(128)}, f32[128,12,64]{0,2,1:T(8,128)}, ...), condition=%wide.region_63.64_spmd.clone, body=%wide.region_60.63_spmd.clone.sunk | while | flops 512361088 | bytes 32499304 | solution.py:333
  604.2 4.7 conditional.44
  639.1 17.8 %reduce-scatter.50.cloned.1.call-done = bf16[128,768]{1,0:T(8,128)(2,1)} async-done(((bf16[1024,768]{1,0:T(8,128)(2,1)}), bf16[128,768]{1,0:T(8,128)(2,1)}) %reduce-scatter.50.cloned.1.call-update) | async-done | bytes 196624
  658.9 32.6 %reduce-scatter.46.cloned.1.call-done = bf16[128,768]{1,0:T(8,128)(2,1)} async-done(((bf16[1024,768]{1,0:T(8,128)(2,1)}), bf16[128,768]{1,0:T(8,128)(2,1)}) %reduce-scatter.46.cloned.1.call-update) | async-done | bytes 196624
  704.8 21.5 %reduce-scatter.56.cloned.1.call-done = bf16[128,768]{1,0:T(8,128)(2,1)} async-done(((bf16[1024,768]{1,0:T(8,128)(2,1)}), bf16[128,768]{1,0:T(8,128)(2,1)}) %reduce-scatter.56.cloned.1.call-update) | async-done | bytes 196624
  727.8 33.1 %reduce-scatter.48.cloned.1.call-done = bf16[128,768]{1,0:T(8,128)(2,1)} async-done(((bf16[1024,768]{1,0:T(8,128)(2,1)}), bf16[128,768]{1,0:T(8,128)(2,1)}) %reduce-scatter.48.cloned.1.call-update) | async-done | bytes 196624
  763.7 31.7 %reduce-scatter.52.cloned.1.call-done = bf16[128,768]{1,0:T(8,128)(2,1)} async-done(((bf16[1024,768]{1,0:T(8,128)(2,1)}), bf16[128,768]{1,0:T(8,128)(2,1)}) %reduce-scatter.52.cloned.1.call-update) | async-done | bytes 196624
  798.2 32.3 %reduce-scatter.60.cloned.1.call-done = bf16[128,768]{1,0:T(8,128)(2,1)} async-done(((bf16[1024,768]{1,0:T(8,128)(2,1)}), bf16[128,768]{1,0:T(8,128)(2,1)}) %reduce-scatter.60.cloned.1.call-update) | async-done | bytes 196624
  830.5 3.9 fusion.214
  862.4 10.0 all-reduce.6
  872.6 13.6 %all-reduce.4 = (bf16[192]{0:T(256)(128)(2,1)S(1)}, bf16[192]{0:T(256)(128)(2,1)S(1)}) all-reduce(bf16[192]{0:T(256)(128)(2,1)S(1)} %dynamic-slice.3, bf16[192]{0:T(256)(128)(2,1)S(1)} %dynamic-slice.5), channel_id=1, replica_groups=mesh['seq'=8,'fsdp'=4] {'seq'}, use_global_device_ids=true, to_apply=%region_112.113 | all-reduce | flops 384 | bytes 1536 | tf_op jit(solution)/shard_map/psum | solution.py:404
  898.4 25.3 %reduce-scatter.66.cloned.1.call-done = bf16[192,768]{1,0:T(8,128)(2,1)} async-done(((bf16[768,768]{1,0:T(8,128)(2,1)}), bf16[192,768]{1,0:T(8,128)(2,1)}) %reduce-scatter.66.cloned.1.call-update) | async-done | bytes 294928
  925.6 30.0 %reduce-scatter.38.cloned.1.call-done = bf16[192,768]{1,0:T(8,128)(2,1)} async-done(((bf16[768,768]{1,0:T(8,128)(2,1)}), bf16[192,768]{1,0:T(8,128)(2,1)}) %reduce-scatter.38.cloned.1.call-update) | async-done | bytes 294928 | tf_op jit(solution)/shard_map/reduce_scatter | solution.py:401
  955.7 47.0 %reduce-scatter.40.cloned.1.call-done = bf16[192,2048]{1,0:T(8,128)(2,1)} async-done(((bf16[768,2048]{1,0:T(8,128)(2,1)}), bf16[192,2048]{1,0:T(8,128)(2,1)}) %reduce-scatter.40.cloned.1.call-update) | async-done | bytes 786448 | tf_op jit(solution)/shard_map/reduce_scatter | solution.py:401
  1002.7 47.0 %reduce-scatter.42.cloned.1.call-done = bf16[192,2048]{1,0:T(8,128)(2,1)} async-done(((bf16[768,2048]{1,0:T(8,128)(2,1)}), bf16[192,2048]{1,0:T(8,128)(2,1)}) %reduce-scatter.42.cloned.1.call-update) | async-done | bytes 786448 | tf_op jit(solution)/shard_map/reduce_scatter | solution.py:401
  1049.6 46.8 %reduce-scatter.44.cloned.1.call-done = bf16[512,768]{1,0:T(8,128)(2,1)} async-done(((bf16[2048,768]{1,0:T(8,128)(2,1)}), bf16[512,768]{1,0:T(8,128)(2,1)}) %reduce-scatter.44.cloned.1.call-update) | async-done | bytes 786448 | tf_op jit(solution)/shard_map/reduce_scatter | solution.py:401
  1103.6 88.7 %all-reduce.10.cloned.1.call-done = (bf16[192,768]{0,1:T(8,128)(2,1)}, bf16[192,768]{0,1:T(8,128)(2,1)}, bf16[192,768]{0,1:T(8,128)(2,1)}, bf16[192,768]{1,0:T(8...) async-done(((bf16[192,768]{0,1:T(8,128)(2,1)}, bf16[192,768]{0,1:T(8,128)(2,1)}, bf16[192,768]{0,1:T(8,128)(2,1)}, ...) | async-done | bytes 3538960 | tf_op jit(solution)/shard_map/psum | solution.py:404
  (1004 shorter events, 356.4 us)
Async XLA Ops:
  7.2 33.1 %all-gather.20.cloned.1.call-start = ((), (), s32[]{:S(2)}) async-start(), calls=%async_computation.17 | async-start | bytes 1474560 | tf_op jit(solution)/shard_map/all_gather | solution.py:211
  7.9 62.0 %all-gather.16.cloned.1.call-start = ((), (), s32[]{:S(2)}) async-start(), calls=%async_computation.15 | async-start | bytes 1474560 | tf_op jit(solution)/shard_map/all_gather | solution.py:212
  8.7 90.8 %all-gather.22.cloned.1.call-start = ((), (), s32[]{:S(2)}) async-start(), calls=%async_computation.18 | async-start | bytes 1474560 | tf_op jit(solution)/shard_map/all_gather | solution.py:213
  9.4 124.7 %all-gather.18.cloned.1.call-start = ((), (), s32[]{:S(2)}) async-start(), calls=%async_computation.16 | async-start | bytes 1769472 | tf_op jit(solution)/shard_map/all_gather | solution.py:249
  22.6 52.0 %copy-start.154 = (f32[128,64]{0,1:T(8,128)}, f32[128,64]{0,1:T(8,128)S(1)}, u32[]{:S(2)}) copy-start(f32[128,64]{0,1:T(8,128)S(1)} %get-tuple-element.5350) | copy-start | bytes 98308
  22.6 52.0 %copy-start.166 = (f32[128,64]{0,1:T(8,128)}, f32[128,64]{0,1:T(8,128)S(1)}, u32[]{:S(2)}) copy-start(f32[128,64]{0,1:T(8,128)S(1)} %get-tuple-element.5351) | copy-start | bytes 98308
  40.3 32.0 %copy-start.23 = (bf16[4,1,128,768]{3,2,1,0:T(8,128)(2,1)S(1)}, bf16[4,1,128,768]{3,2,1,0:T(8,128)(2,1)}, u32[]{:S(2)}) copy-start(bf16[4,1,128,768]{3,2,1,0:T(8,128)(2,1)} %param.60) | copy-start | bytes 2359300
  42.0 60.0 %copy-start.28 = (bf16[768,768]{1,0:T(8,128)(2,1)}, bf16[768,768]{1,0:T(8,128)(2,1)S(1)}, u32[]{:S(2)}) copy-start(bf16[768,768]{1,0:T(8,128)(2,1)S(1)} %copy.201) | copy-start | bytes 3538948
  75.4 79.6 %all-gather.24.cloned.1.call-start = ((), (), s32[]{:S(2)}) async-start(), calls=%async_computation.19 | async-start | bytes 1769472 | tf_op jit(solution)/shard_map/all_gather | solution.py:250
  101.8 82.0 %all-gather.34.cloned.1.call-start = ((), (), s32[]{:S(2)}) async-start(), calls=%async_computation.24 | async-start | bytes 1769472 | tf_op jit(solution)/shard_map/all_gather | solution.py:249
  105.2 105.0 %all-gather.36.cloned.1.call-start = ((), (), s32[]{:S(2)}) async-start(), calls=%async_computation.25 | async-start | bytes 1769472 | tf_op jit(solution)/shard_map/all_gather | solution.py:250
  106.3 132.8 %all-gather.38.cloned.1.call-start = ((), (), s32[]{:S(2)}) async-start(), calls=%async_computation.26 | async-start | bytes 1769472 | tf_op jit(solution)/shard_map/all_gather | solution.py:249
  110.9 154.7 %all-gather.40.cloned.1.call-start = ((), (), s32[]{:S(2)}) async-start(), calls=%async_computation.27 | async-start | bytes 1769472 | tf_op jit(solution)/shard_map/all_gather | solution.py:250
  112.0 181.9 %all-gather.42.cloned.1.call-start = ((), (), s32[]{:S(2)}) async-start(), calls=%async_computation.28 | async-start | bytes 1769472 | tf_op jit(solution)/shard_map/all_gather | solution.py:249
  116.7 202.9 %all-gather.44.cloned.1.call-start = ((), (), s32[]{:S(2)}) async-start(), calls=%async_computation.29 | async-start | bytes 1769472 | tf_op jit(solution)/shard_map/all_gather | solution.py:250
  117.8 230.8 %all-gather.26.cloned.1.call-start = ((), (), s32[]{:S(2)}) async-start(), calls=%async_computation.20 | async-start | bytes 1474560 | tf_op jit(solution)/shard_map/all_gather | solution.py:214
  118.4 276.1 %all-gather.28.cloned.1.call-start = ((), (), s32[]{:S(2)}) async-start(), calls=%async_computation.21 | async-start | bytes 3932160 | tf_op jit(solution)/shard_map/all_gather | solution.py:215
  119.2 321.0 %all-gather.30.cloned.1.call-start = ((), (), s32[]{:S(2)}) async-start(), calls=%async_computation.22 | async-start | bytes 3932160 | tf_op jit(solution)/shard_map/all_gather | solution.py:216
  119.7 366.2 %all-gather.32.cloned.1.call-start = ((), (), s32[]{:S(2)}) async-start(), calls=%async_computation.23 | async-start | bytes 3932160 | tf_op jit(solution)/shard_map/all_gather | solution.py:217
  120.3 514.6 %reduce-scatter.58.cloned.1.call-start = ((), (), s32[]{:S(2)}) async-start(), calls=%async_computation.40 | async-start | bytes 1769472
  132.1 383.2 %copy-start.164 = (f32[768]{0:T(1024)}, f32[768]{0:T(1024)S(1)}, u32[]{:S(2)}) copy-start(f32[768]{0:T(1024)S(1)} %convert_element_type.627) | copy-start | bytes 9220
  351.5 45.4 %copy-start.41 = (f32[128,768]{1,0:T(8,128)}, f32[128,768]{1,0:T(8,128)S(1)}, u32[]{:S(2)}) copy-start(f32[128,768]{1,0:T(8,128)S(1)} %get-tuple-element.5389) | copy-start | bytes 1179652
  351.6 42.9 %copy-start.197 = (f32[128]{0:T(128)}, f32[128]{0:T(128)S(1)}, u32[]{:S(2)}) copy-start(f32[128]{0:T(128)S(1)} %add_rsqrt_fusion.3) | copy-start | bytes 1540
  352.0 45.0 %copy-start.43 = (f32[128,768]{1,0:T(8,128)}, f32[128,768]{1,0:T(8,128)S(1)}, u32[]{:S(2)}) copy-start(f32[128,768]{1,0:T(8,128)S(1)} %get-tuple-element.5391) | copy-start | bytes 1179652
  352.1 44.9 %copy-start.199 = (f32[128]{0:T(128)}, f32[128]{0:T(128)S(1)}, u32[]{:S(2)}) copy-start(f32[128]{0:T(128)S(1)} %add_rsqrt_fusion.1) | copy-start | bytes 1540
  353.1 87.1 %copy-start.93 = (bf16[128,768]{1,0:T(8,128)(2,1)}, bf16[128,768]{1,0:T(8,128)(2,1)S(1)}, u32[]{:S(2)}) copy-start(bf16[128,768]{1,0:T(8,128)(2,1)S(1)} %get-tuple-element.5369) | copy-start | bytes 589828
  397.0 43.2 %copy-start.139 = (f32[128,2048]{1,0:T(8,128)}, f32[128,2048]{1,0:T(8,128)S(1)}, u32[]{:S(2)}) copy-start(f32[128,2048]{1,0:T(8,128)S(1)} %fusion.399) | copy-start | bytes 3145732
  443.9 44.8 %copy-start = (bf16[768,2048]{1,0:T(8,128)(2,1)S(1)}, bf16[768,2048]{1,0:T(8,128)(2,1)}, u32[]{:S(2)}) copy-start(bf16[768,2048]{1,0:T(8,128)(2,1)} %all-gather.28.cloned.1.call-done) | copy-start | bytes 9437188
  548.1 89.0 %reduce-scatter.54.cloned.1.call-start = ((), (), s32[]{:S(2)}) async-start(), calls=%async_computation.38 | async-start | bytes 1769472
  574.0 83.0 %reduce-scatter.50.cloned.1.call-start = ((), (), s32[]{:S(2)}) async-start(), calls=%async_computation.36 | async-start | bytes 1769472
  596.8 94.7 %reduce-scatter.46.cloned.1.call-start = ((), (), s32[]{:S(2)}) async-start(), calls=%async_computation.34 | async-start | bytes 1769472
  619.4 106.9 %reduce-scatter.56.cloned.1.call-start = ((), (), s32[]{:S(2)}) async-start(), calls=%async_computation.39 | async-start | bytes 1769472
  623.1 137.7 %reduce-scatter.48.cloned.1.call-start = ((), (), s32[]{:S(2)}) async-start(), calls=%async_computation.35 | async-start | bytes 1769472
  626.9 168.5 %reduce-scatter.52.cloned.1.call-start = ((), (), s32[]{:S(2)}) async-start(), calls=%async_computation.37 | async-start | bytes 1769472
  631.1 199.4 %reduce-scatter.60.cloned.1.call-start = ((), (), s32[]{:S(2)}) async-start(), calls=%async_computation.41 | async-start | bytes 1769472
  634.8 259.8 %reduce-scatter.62.cloned.1.call-start = ((), (), s32[]{:S(2)}) async-start(), calls=%async_computation.42 | async-start | bytes 1474560
  637.1 65.6 %copy-start.120 = (bf16[128,768]{0,1:T(8,128)(2,1)}, bf16[128,768]{0,1:T(8,128)(2,1)S(1)}, u32[]{:S(2)}) copy-start(bf16[128,768]{0,1:T(8,128)(2,1)S(1)} %fusion.267) | copy-start | bytes 589828
  638.3 54.4 %copy-start.31 = (f32[128,12,64]{0,2,1:T(8,128)S(1)}, f32[128,12,64]{0,2,1:T(8,128)}, u32[]{:S(2)}) copy-start(f32[128,12,64]{0,2,1:T(8,128)} %get-tuple-element.3975) | copy-start | bytes 1179652
  699.1 197.4 %reduce-scatter.64.cloned.1.call-start = ((), (), s32[]{:S(2)}) async-start(), calls=%async_computation.43 | async-start | bytes 1474560
  704.6 219.2 %reduce-scatter.66.cloned.1.call-start = ((), (), s32[]{:S(2)}) async-start(), calls=%async_computation.44 | async-start | bytes 1474560
  836.9 118.7 %reduce-scatter.38.cloned.1.call-start = ((), (), s32[]{:S(2)}) async-start(), calls=%async_computation.30 | async-start | bytes 1474560 | tf_op jit(solution)/shard_map/reduce_scatter | solution.py:401
  840.6 162.1 %reduce-scatter.40.cloned.1.call-start = ((), (), s32[]{:S(2)}) async-start(), calls=%async_computation.31 | async-start | bytes 3932160 | tf_op jit(solution)/shard_map/reduce_scatter | solution.py:401
  846.8 202.8 %reduce-scatter.42.cloned.1.call-start = ((), (), s32[]{:S(2)}) async-start(), calls=%async_computation.32 | async-start | bytes 3932160 | tf_op jit(solution)/shard_map/reduce_scatter | solution.py:401
  853.8 242.7 %reduce-scatter.44.cloned.1.call-start = ((), (), s32[]{:S(2)}) async-start(), calls=%async_computation.33 | async-start | bytes 3932160 | tf_op jit(solution)/shard_map/reduce_scatter | solution.py:401
  861.4 25.9 %copy-start.141 = (bf16[1,128,768]{2,1,0:T(8,128)(2,1)S(1)}, bf16[1,128,768]{2,1,0:T(8,128)(2,1)}, u32[]{:S(2)}) copy-start(bf16[1,128,768]{2,1,0:T(8,128)(2,1)} %get-tuple-element.5298) | copy-start | bytes 589828
  861.5 26.8 %copy-start.26 = (bf16[768,768]{1,0:T(8,128)(2,1)S(1)}, bf16[768,768]{1,0:T(8,128)(2,1)}, u32[]{:S(2)}) copy-start(bf16[768,768]{1,0:T(8,128)(2,1)} %all-gather.20.cloned.1.call-done) | copy-start | bytes 3538948
  861.5 28.5 %copy-start.27 = (bf16[768,768]{1,0:T(8,128)(2,1)S(1)}, bf16[768,768]{1,0:T(8,128)(2,1)}, u32[]{:S(2)}) copy-start(bf16[768,768]{1,0:T(8,128)(2,1)} %all-gather.16.cloned.1.call-done) | copy-start | bytes 3538948
  861.5 330.7 %all-reduce.10.cloned.1.call-start = ((), (), s32[]{:S(2)}) async-start(), calls=%async_computation.45 | async-start | bytes 7667712 | tf_op jit(solution)/shard_map/psum | solution.py:404
  (219 other events, 806.7 us)
Sparse Core Ops, SparseCore 0:
  9.8 30.4 all-gather.19
  42.1 27.7 all-gather.15
  71.8 27.7 all-gather.21
  101.5 27.1 all-gather.17
  130.8 24.2 all-gather.23
  157.1 26.6 all-gather.33
  186.0 24.2 all-gather.35
  212.4 26.6 all-gather.37
  241.4 24.1 all-gather.39
  267.0 26.8 all-gather.41
  295.6 24.0 all-gather.43
  321.4 27.2 all-gather.25
  350.5 43.9 all-gather.27
  396.2 43.9 all-gather.29
  441.9 43.9 all-gather.31
  548.2 39.8 reduce-scatter.57
  590.2 32.0 reduce-scatter.53
  624.5 32.4 reduce-scatter.49
  659.2 32.1 reduce-scatter.45
  694.2 32.1 reduce-scatter.55
  728.7 32.1 reduce-scatter.47
  763.2 32.1 reduce-scatter.51
  798.3 32.1 reduce-scatter.59
  833.8 26.4 reduce-scatter.61
  863.3 28.5 reduce-scatter.63
  895.2 28.5 reduce-scatter.65
  927.1 28.5 reduce-scatter.37
  958.7 43.9 reduce-scatter.39
  1005.6 43.9 reduce-scatter.41
  1052.5 43.9 reduce-scatter.43
  1100.0 92.2 all-reduce.9
where the time goes:
time: 1220 us; the launch traced here: 1210 us
  waiting for transfers between devices  756 us (62%)
  local copies, waits for them, and re-layouts  169 us (14%)
  matrix products  133 us (11%)
  loops' own time  49.1 us (4%)
  blocking collectives  43.6 us (4%)
  other arithmetic  37.7 us (3%)
  between operations  19.5 us (2%)
    unnamed x42, waiting for transfers between devices  199 us
    reduce_scatter x4, waiting for transfers between devices, body(): lax.psum_scatter(for_sending(summed), 'fsdp', scatter_dimension=0, tiled=...  171 us
    psum x1, waiting for transfers between devices, body(): lax.psum(for_sending(owned_sums), 'seq')  88.7 us
    all_gather x4, waiting for transfers between devices, body(): lax.all_gather(values_own, 'seq', axis=0, tiled=True)  77.3 us
    unnamed x462, local copies, waits for them, and re-layouts  67.5 us
    all_gather x1, waiting for transfers between devices, body(): lax.all_gather(w_up, 'fsdp', axis=0, tiled=True)  43.2 us
    all_gather x1, waiting for transfers between devices, body(): lax.all_gather(w_down, 'fsdp', axis=0, tiled=True)  42 us
    all_gather x1, waiting for transfers between devices, body(): lax.all_gather(w_gate, 'fsdp', axis=0, tiled=True)  41.4 us
  transfers between devices with their start and end apart: 31, of which 26 were waited for; matrix products, arithmetic and copies ran while one was open for 22% of the time, Pallas kernels for 0%

commit v1 on v0

v1 whole, which is shorter than its diff:
```python
import math

import jax
import jax.numpy as jnp
from jax import lax
from jax.experimental import pallas as pl
from jax.experimental.pallas import tpu as pltpu
from jax.sharding import Mesh, PartitionSpec as P

HEADS = 12
DOCS = 4
EPS = 1e-06
NEGATIVE = -1e30
BF = jnp.bfloat16
F32 = jnp.float32


def dot(left, right, dims=((1,), (0,))):
    return lax.dot_general(left, right, (dims, ((), ())), preferred_element_type=F32)


def rotary_tables(seq_tokens, head_size, copies):
    half = head_size // 2
    frequency = 10000.0 ** (-jnp.arange(half, dtype=F32) / half)
    angle = jnp.arange(seq_tokens, dtype=jnp.int32).astype(F32)[:, None] * frequency[None, :]
    cosine, sine = jnp.cos(angle), jnp.sin(angle)
    return (
        jnp.concatenate([cosine, cosine] * copies, axis=1),
        jnp.concatenate([-sine, sine] * copies, axis=1),
    )


def turn(rows, half):
    lanes = rows.shape[1]
    lane = lax.broadcasted_iota(jnp.int32, (1, lanes), 1)
    low = (lane // half) % 2 == 0
    return jnp.where(low, pltpu.roll(rows, lanes - half, 1), pltpu.roll(rows, half, 1))


def first_key(query_first, block, window):
    return max(0, (query_first - window + 1) // block * block)


def start_row(seg_ref):
    seg = seg_ref[...]
    starts = jnp.zeros_like(seg)
    for doc in range(1, DOCS):
        before = jnp.sum(jnp.where(seg < doc, 1.0, 0.0), axis=1, keepdims=True)
        starts = jnp.maximum(starts, jnp.where(seg >= doc, before, 0.0))
    return starts


def attend_kernel(seg_ref, x_ref, w_ref, cos_ref, sin_ref, q_ref, k_ref, v_ref, att_ref, lse_ref,
                  col_ref, *, block, window, scale, head_size):
    tokens = x_ref.shape[0]
    lane = lax.broadcasted_iota(jnp.int32, (1, 2 * head_size), 1)
    first = lane < head_size

    @pl.when(pl.program_id(0) == 0)
    def _():
        starts = start_row(seg_ref)
        col_ref[...] = jnp.broadcast_to(starts, (128, tokens)).T

    for low in range(0, tokens, block):
        rows = pl.ds(low, block)
        lin = [dot(x_ref[rows, :], w_ref[n]) for n in range(3)]
        cosine, sine = cos_ref[rows, :], sin_ref[rows, :]
        half = head_size // 2
        q_ref[rows, :] = (lin[0] * cosine + turn(lin[0], half) * sine).astype(BF)
        k_ref[rows, :] = (lin[1] * cosine + turn(lin[1], half) * sine).astype(BF)
        v_ref[rows, :] = lin[2].astype(BF)
    for low in range(0, tokens, block):
        begin = first_key(low, block, window)
        end = low + block
        q = q_ref[low:end, :] * jnp.asarray(scale, BF)
        zero = jnp.zeros_like(q)
        stacked = jnp.concatenate([jnp.where(first, q, zero), jnp.where(first, zero, q)], axis=0)
        scores = dot(stacked, k_ref[begin:end, :], ((1,), (1,)))
        key_index = lax.broadcasted_iota(jnp.int32, (block, end - begin), 1) + begin
        query_index = lax.broadcasted_iota(jnp.int32, (block, end - begin), 0) + low
        visible = (key_index.astype(F32) >= col_ref[low:end, 0:1]) & (key_index <= query_index)
        parts = []
        for head in range(2):
            own = jnp.where(visible, scores[head * block:(head + 1) * block], NEGATIVE)
            top = jnp.max(own, axis=1, keepdims=True)
            weights = jnp.exp(own - top)
            total = jnp.sum(weights, axis=1, keepdims=True)
            out = dot(weights.astype(BF), v_ref[begin:end, :]) / total
            parts.append(out)
            lse = jnp.broadcast_to(top + jnp.log(total), (block, 128))
            lse_ref[0, head:head + 1, low:end] = lse.T[0:1, :]
        att_ref[low:end, :] = jnp.where(first, parts[0], parts[1]).astype(BF)


def attend(seg, x, w, cosine, sine, window, head_size):
    tokens, width = x.shape
    pairs = w.shape[2] // (2 * head_size)
    lanes = 2 * head_size
    block = 256
    kernel = lambda *refs: attend_kernel(
        *refs, block=block, window=window, scale=1.0 / math.sqrt(head_size), head_size=head_size)
    whole = lambda p: (0, 0)
    column = pl.BlockSpec((tokens, lanes), lambda p: (0, p))
    flops = 2 * tokens * (width * 3 + 4 * window) * lanes * pairs
    return pl.pallas_call(
        kernel,
        grid=(pairs,),
        in_specs=[
            pl.BlockSpec((1, tokens), whole),
            pl.BlockSpec((tokens, width), whole),
            pl.BlockSpec((3, width, lanes), lambda p: (0, 0, p)),
            pl.BlockSpec((tokens, lanes), whole),
            pl.BlockSpec((tokens, lanes), whole),
        ],
        out_specs=[column, column, column, column, pl.BlockSpec((1, 8, tokens), lambda p: (p, 0, 0))],
        out_shape=[jax.ShapeDtypeStruct((tokens, lanes * pairs), BF)] * 4
        + [jax.ShapeDtypeStruct((pairs, 8, tokens), F32)],
        scratch_shapes=[pltpu.VMEM((tokens, 128), F32)],
        compiler_params=pltpu.CompilerParams(vmem_limit_bytes=40 << 20),
        cost_estimate=pl.CostEstimate(flops=flops, bytes_accessed=8 << 20, transcendentals=0),
        name="attend",
    )(seg, x, w, cosine, sine)


def attend_back_kernel(seg_ref, g_ref, w_ref, q_ref, k_ref, v_ref, att_ref, lse_ref, cos_ref, sin_ref,
                       dq_ref, dk_ref, dv_ref, grad_ref, k_sum, v_sum, *, block, window, scale, head_size):
    tokens = g_ref.shape[0]
    half = head_size // 2
    lane = lax.broadcasted_iota(jnp.int32, (1, 2 * head_size), 1)
    first = lane < head_size
    starts = start_row(seg_ref)
    k_sum[...] = jnp.zeros_like(k_sum)
    v_sum[...] = jnp.zeros_like(v_sum)
    for low in range(0, tokens, block):
        rows = pl.ds(low, block)
        grad_ref[rows, :] = dot(g_ref[rows, :], w_ref[...], ((1,), (1,))).astype(BF)
    for low in range(0, tokens, block):
        begin = first_key(low, block, window)
        end = low + block
        count = end - begin
        q = q_ref[low:end, :] * jnp.asarray(scale, BF)
        grad = grad_ref[low:end, :]
        product = (grad.astype(F32) * att_ref[low:end, :].astype(F32)).T
        k = k_ref[begin:end, :]
        v = v_ref[begin:end, :]
        zero = jnp.zeros_like(k)
        k_two = jnp.concatenate([jnp.where(first, k, zero), jnp.where(first, zero, k)], axis=0)
        v_two = jnp.concatenate([jnp.where(first, v, zero), jnp.where(first, zero, v)], axis=0)
        scores = dot(k_two, q, ((1,), (1,)))
        prob_grad = dot(v_two, grad, ((1,), (1,)))
        key_index = lax.broadcasted_iota(jnp.int32, (count, block), 0) + begin
        query_index = lax.broadcasted_iota(jnp.int32, (count, block), 1) + low
        visible = (key_index.astype(F32) >= starts[:, low:end]) & (key_index <= query_index)
        weights_low, score_low = [], []
        for head in range(2):
            part = slice(head * count, (head + 1) * count)
            weights = jnp.where(
                visible, jnp.exp(scores[part] - lse_ref[0, head:head + 1, low:end]), 0.0)
            row_dots = jnp.sum(
                product[head * head_size:(head + 1) * head_size], axis=0, keepdims=True)
            weights_low.append(weights.astype(BF))
            score_low.append((weights * (prob_grad[part] - row_dots)).astype(BF))
        weights_low = jnp.concatenate(weights_low, axis=0)
        score_low = jnp.concatenate(score_low, axis=0)
        v_part = dot(weights_low, grad)
        k_part = dot(score_low, q)
        v_sum[begin:end, :] += jnp.where(first, v_part[:count], v_part[count:])
        k_sum[begin:end, :] += jnp.where(first, k_part[:count], k_part[count:])
        dq = dot(score_low, k_two, ((0,), (0,))) * scale
        dq_ref[low:end, :] = (
            dq * cos_ref[low:end, :] - turn(dq, half) * sin_ref[low:end, :]).astype(BF)
    for low in range(0, tokens, block):
        rows = pl.ds(low, block)
        dk = k_sum[rows, :]
        dk_ref[rows, :] = (dk * cos_ref[rows, :] - turn(dk, half) * sin_ref[rows, :]).astype(BF)
        dv_ref[rows, :] = v_sum[rows, :].astype(BF)


def attend_back(seg, g, w_out, q, k, v, att, lse, cosine, sine, window, head_size):
    tokens, width = g.shape
    lanes = 2 * head_size
    pairs = q.shape[1] // lanes
    block = 256
    kernel = lambda *refs: attend_back_kernel(
        *refs, block=block, window=window, scale=1.0 / math.sqrt(head_size), head_size=head_size)
    whole = lambda p: (0, 0)
    column = pl.BlockSpec((tokens, lanes), lambda p: (0, p))
    flops = 2 * tokens * (width + 10 * window) * lanes * pairs
    return pl.pallas_call(
        kernel,
        grid=(pairs,),
        in_specs=[
            pl.BlockSpec((1, tokens), whole),
            pl.BlockSpec((tokens, width), whole),
            pl.BlockSpec((lanes, width), lambda p: (p, 0)),
            column, column, column, column,
            pl.BlockSpec((1, 8, tokens), lambda p: (p, 0, 0)),
            pl.BlockSpec((tokens, lanes), whole),
            pl.BlockSpec((tokens, lanes), whole),
        ],
        out_specs=[column, column, column],
        out_shape=[jax.ShapeDtypeStruct((tokens, lanes * pairs), BF)] * 3,
        scratch_shapes=[
            pltpu.VMEM((tokens, lanes), BF),
            pltpu.VMEM((tokens, lanes), F32),
            pltpu.VMEM((tokens, lanes), F32),
        ],
        compiler_params=pltpu.CompilerParams(vmem_limit_bytes=48 << 20),
        cost_estimate=pl.CostEstimate(flops=flops, bytes_accessed=8 << 20, transcendentals=0),
        name="attend_back",
    )(seg, g, w_out, q, k, v, att, lse, cosine, sine)


def normalize(rows, gain):
    factor = lax.rsqrt(jnp.mean(rows * rows, axis=-1, keepdims=True) + EPS)
    unit = rows * factor
    return unit * gain, unit, factor


def normalize_back(grad, unit, factor, gain):
    scaled = grad * gain
    inner = jnp.mean(scaled * unit, axis=-1, keepdims=True)
    return factor * (scaled - unit * inner), jnp.sum(grad * unit, axis=0)


def make_body(groups, ranks, fsdp, square):
    F = ("y", "x") if square else ("f",)
    swap = [(0, 1), (1, 0)]

    def spread(slabs):
        me = lax.axis_index("m")
        out = jnp.zeros_like(slabs)
        for k in range(groups):
            slab = lax.dynamic_index_in_dim(slabs, me ^ k, 0, keepdims=False)
            if k:
                slab = lax.ppermute(slab, "m", [(i, i ^ k) for i in range(groups)])
            out = lax.dynamic_update_index_in_dim(out, slab, me ^ k, 0)
        return out

    def share(part):
        if ranks == 2:
            other = lax.ppermute(part, "r", swap)
            mine_first = lax.axis_index("r") == 0
            return jnp.stack(
                [jnp.where(mine_first, part, other), jnp.where(mine_first, other, part)], axis=1)
        return lax.all_gather(part, "r", axis=1)

    def total(part):
        if ranks == 2:
            return part + lax.ppermute(part.astype(BF), "r", swap).astype(F32)
        return lax.psum(part.astype(BF), "r").astype(F32)

    def gather_rows(part):
        if not square:
            return lax.all_gather(part, F, axis=0)
        rows = part.shape[0] // 2
        me = lax.axis_index(F)
        from_x = lax.ppermute(part, "x", swap)
        from_y = lax.ppermute(part, "y", swap)
        far_a = lax.ppermute(from_y[:rows], "x", swap)
        far_b = lax.ppermute(from_x[rows:], "y", swap)
        out = jnp.zeros((fsdp,) + part.shape, part.dtype)
        out = lax.dynamic_update_index_in_dim(out, part, me, 0)
        out = lax.dynamic_update_index_in_dim(out, from_x, me ^ 1, 0)
        out = lax.dynamic_update_index_in_dim(out, from_y, me ^ 2, 0)
        out = lax.dynamic_update_slice(out, far_a[None], (me ^ 3, 0, 0))
        return lax.dynamic_update_slice(out, far_b[None], (me ^ 3, rows, 0))

    def body(tokens, segments, w_query, w_key, w_value, w_out, w_gate, w_up, w_down,
             gain_attn, gain_ffn, cotangent):
        micro, _, span, width = tokens.shape
        head_size = width // HEADS
        seq_tokens = span * groups * ranks
        window = seq_tokens // 2
        rank = lax.axis_index("r")
        own_cols = width // ranks
        shard = w_query.shape[0]
        down_rows = w_down.shape[0]
        part_rows = down_rows // ranks
        ff = w_gate.shape[1]

        def columns(w):
            return lax.dynamic_slice_in_dim(w, rank * own_cols, own_cols, 1)

        def ff_columns(w):
            return lax.dynamic_slice_in_dim(
                w.reshape(shard, fsdp, down_rows), rank * part_rows, part_rows, 2
            ).reshape(shard, ff // ranks)

        small = jnp.concatenate([columns(w) for w in (w_query, w_key, w_value, w_out)], axis=1)
        seg_rows = jnp.pad(segments[:, 0, None, :].astype(BF), ((0, 0), (0, 15), (0, width - span)))
        token_slabs = jnp.concatenate([tokens[:, 0], seg_rows], axis=1)

        mine = spread(token_slabs)
        small_all = gather_rows(small).reshape(width, 4 * own_cols)
        gate_up = jnp.concatenate([ff_columns(w_gate), ff_columns(w_up)], axis=1)
        down = lax.dynamic_slice_in_dim(w_down, rank * part_rows, part_rows, 0)
        gu_all = lax.all_gather(gate_up, F, axis=0, tiled=True)
        down_all = lax.all_gather(down, F, axis=0, tiled=True)
        gains = lax.all_gather(jnp.stack([gain_attn, gain_ffn]), F, axis=1, tiled=True).astype(F32)
        gain_one, gain_two = gains[0], gains[1]
        cot_mine = spread(cotangent[:, 0])

        both = share(mine)
        x = both[:, :, :span].reshape(seq_tokens, width)
        seg = both[:, :, span, :span].reshape(1, seq_tokens).astype(F32)
        cosine, sine = rotary_tables(seq_tokens, head_size, 2)
        w_qkv = jnp.stack([small_all[:, n * own_cols:(n + 1) * own_cols] for n in range(3)])
        spare = -own_cols % (2 * head_size)
        out_cols = small_all[:, 3 * own_cols:]
        if ranks == 2:
            give = lax.dynamic_slice_in_dim(out_cols, (1 - rank) * own_cols, own_cols, 0)
            keep = lax.dynamic_slice_in_dim(out_cols, rank * own_cols, own_cols, 0)
            got = lax.ppermute(give, "r", swap)
            w_out_own = jnp.where(rank == 0, jnp.concatenate([keep, got], 1),
                                  jnp.concatenate([got, keep], 1))
        else:
            pieces = lax.all_to_all(out_cols, "r", 0, 0, tiled=True)
            pieces = pieces.reshape(ranks, own_cols, own_cols)
            w_out_own = jnp.concatenate([pieces[i] for i in range(ranks)], axis=1)

        w_qkv_even = jnp.pad(w_qkv, ((0, 0), (0, 0), (0, spare)))
        w_out_even = jnp.pad(w_out_own, ((0, spare), (0, 0)))
        q, k, v, att_even, lse = attend(seg, x, w_qkv_even, cosine, sine, window, head_size)
        att = att_even[:, :own_cols]
        branch = total(dot(att, w_out_own))
        middle, unit_one, factor_one = normalize(x.astype(F32) + branch, gain_one)
        middle_low = middle.astype(BF)
        half_ff = ff // ranks
        gate_up_pre = dot(middle_low, gu_all)
        gate_pre, up_pre = gate_up_pre[:, :half_ff], gate_up_pre[:, half_ff:]
        gate_sig = jax.nn.sigmoid(gate_pre)
        gate_silu = gate_pre * gate_sig
        hidden_low = (gate_silu * up_pre).astype(BF)
        ffn_out = total(dot(hidden_low, down_all))
        result, unit_two, factor_two = normalize(middle + ffn_out, gain_two)

        def own_tokens(rows):
            rows = rows.reshape(groups, ranks, span, width)
            return lax.dynamic_index_in_dim(rows, rank, 1, keepdims=False)

        output = spread(own_tokens(result.astype(BF)))
        cot = share(cot_mine).reshape(seq_tokens, width).astype(F32)
        ffn_grad, gain_ffn_grad = normalize_back(cot, unit_two, factor_two, gain_two)
        ffn_grad_low = ffn_grad.astype(BF)
        down_w_grad = dot(hidden_low, ffn_grad_low, ((0,), (0,)))
        hidden_grad = dot(ffn_grad_low, down_all, ((1,), (1,)))
        gate_grad = hidden_grad * up_pre * gate_sig * (1.0 + gate_pre * (1.0 - gate_sig))
        up_grad = hidden_grad * gate_silu
        gu_grad_low = jnp.concatenate([gate_grad.astype(BF), up_grad.astype(BF)], axis=1)
        gu_w_grad = dot(middle_low, gu_grad_low, ((0,), (0,)))
        middle_grad = ffn_grad + total(dot(gu_grad_low, gu_all, ((1,), (1,))))
        branch_grad, gain_attn_grad = normalize_back(middle_grad, unit_one, factor_one, gain_one)
        branch_grad_low = branch_grad.astype(BF)
        out_w_grad = dot(att, branch_grad_low, ((0,), (0,)))
        dq, dk, dv = (d[:, :own_cols] for d in attend_back(
            seg, branch_grad_low, w_out_even, q, k, v, att_even, lse, cosine, sine,
            window, head_size))
        part = sum(dot(d, w_qkv[n], ((1,), (1,))) for n, d in enumerate((dq, dk, dv)))
        qkv_w_grad = [dot(x, d, ((0,), (0,))) for d in (dq, dk, dv)]
        if ranks == 2:
            rows = part.reshape(groups, ranks, span, width)
            give = lax.dynamic_index_in_dim(rows, 1 - rank, 1, keepdims=False).astype(BF)
            part_own = own_tokens(part) + lax.ppermute(give, "r", swap).astype(F32)
        else:
            part_own = own_tokens(total(part))
        input_grad = spread((own_tokens(branch_grad) + part_own).astype(BF))

        if ranks == 2:
            low = out_w_grad.astype(BF)
            give = lax.dynamic_slice_in_dim(low, (1 - rank) * own_cols, own_cols, 1)
            keep = lax.dynamic_slice_in_dim(low, rank * own_cols, own_cols, 1)
            got = lax.ppermute(give, "r", swap)
            out_cols_grad = jnp.where(rank == 0, jnp.concatenate([keep, got], 0),
                                      jnp.concatenate([got, keep], 0))
        else:
            low = out_w_grad.astype(BF).reshape(own_cols, ranks, own_cols).transpose(1, 0, 2)
            out_cols_grad = lax.all_to_all(low, "r", 0, 0, tiled=True).reshape(width, own_cols)
        small_grad = jnp.concatenate([g.astype(BF) for g in qkv_w_grad] + [out_cols_grad], axis=1)

        def reduce(grad):
            owned = lax.psum_scatter(grad.astype(BF), F, scatter_dimension=0, tiled=True)
            return lax.psum(owned, "m")

        down_sum = reduce(down_w_grad)
        gu_sum = reduce(gu_w_grad)
        small_sum = reduce(small_grad)
        down_grad = jnp.moveaxis(share(down_sum), 1, 0).reshape(down_rows, width).astype(F32)
        gu_both = share(gu_sum.reshape(shard, 2 * fsdp, part_rows))
        gu_both = gu_both.reshape(shard, ranks, 2, fsdp, part_rows).astype(F32)
        gate_w, up_w = (
            gu_both[:, :, n].transpose(0, 2, 1, 3).reshape(shard, ff) for n in range(2))
        small_both = share(small_sum).reshape(shard, ranks, 4, own_cols).astype(F32)
        query_w, key_w, value_w, out_w = (
            small_both[:, :, n].reshape(shard, width) for n in range(4))
        gain_sums = lax.psum(jnp.stack([gain_attn_grad, gain_ffn_grad]), ("m",) + F)
        gain_own = lax.dynamic_slice_in_dim(gain_sums, lax.axis_index(F) * shard, shard, 1)
        return (output[:, None], input_grad[:, None], query_w, key_w, value_w, out_w,
                gate_w, up_w, down_grad, gain_own[0], gain_own[1])

    return body


def solution(mesh):
    def run(*args):
        groups = args[0].shape[0]
        seq, fsdp = mesh.shape["seq"], mesh.shape["fsdp"]
        ranks = seq // groups
        square = fsdp == 4
        names = ("m", "r") + (("y", "x") if square else ("f",))
        sizes = (groups, ranks) + ((2, 2) if square else (fsdp,))
        order = [mesh.axis_names.index(name) for name in ("seq", "fsdp")]
        inner = Mesh(mesh.devices.transpose(order).reshape(sizes), names)
        f = ("y", "x") if square else "f"
        s = ("m", "r")
        rows = P(f, None)
        data = P(None, f, s, None)
        in_specs = (data, P(None, f, s)) + (rows,) * 7 + (P(f), P(f), data)
        out_specs = (data, data) + (rows,) * 7 + (P(f), P(f))
        body = make_body(groups, ranks, fsdp, square)
        return jax.shard_map(
            body, mesh=inner, in_specs=in_specs, out_specs=out_specs, check_vma=False)(*args)

    return run
```

time: 1220 us -> 392 us (0.32)
  waiting for transfers between devices: 756 us -> 127 us
  local copies, waits for them, and re-layouts: 169 us -> 63.9 us
  matrix products: 133 us -> 42.3 us
  loops' own time: 49.1 us -> 0 us
  Pallas kernels: 0 us -> 27.5 us
  starting transfers between devices: 2.11 us -> 26.6 us
    all_gather x15 -> x2, waiting for transfers between devices: 297 us -> 4.09 us  [the longest x1 4.09 us: body(): down_all = lax.all_gather(down, F, axis=0, tiled=True)]
    unnamed x42 -> x7, waiting for transfers between devices: 199 us -> 30.3 us
    reduce_scatter x4 -> x2, waiting for transfers between devices: 171 us -> 32.2 us  [reduce(): lax.psum_scatter(grad.astype(BF), F, scatter_dimension=0, tiled=True)]
    dot_general x112 -> x14, matrix products: 133 us -> 42.3 us  [dot(): lax.dot_general(left, right, (dims, ((), ())), preferred_element_type=F32)]
    psum x1, waiting for transfers between devices: 88.7 us -> 39.1 us  [reduce(): return lax.psum(owned, 'm')]
    unnamed x462 -> x95, local copies, waits for them, and re-layouts: 67.5 us -> 18.3 us
    another operation x36 -> x0, loops' own time: 49.1 us -> none  [the longest x4 17.5 us: body(): lax.scan(key_step, jnp.zeros((span_rows, head_count, head_size), jnp.floa...]
    pallas_call x0 -> x2, Pallas kernels: none -> 27.5 us  [the longest x1 14.4 us: attend_back(): pl.pallas_call(kernel, grid=(pairs,), in_specs=[pl.BlockSpec((1, tokens),...]
  transfers between devices with their start and end apart: 31 -> 33, of which waited for: 26 -> 10; matrix products, arithmetic and copies ran while one was open for 22% -> 24% of each run, Pallas kernels for 0% -> 7%
where the time goes in v1:
time: 392 us; the launch traced here: 387 us
  waiting for transfers between devices  127 us (32%)
  local copies, waits for them, and re-layouts  63.9 us (16%)
  blocking collectives  52.1 us (13%)
  matrix products  42.3 us (11%)
  other arithmetic  32.3 us (8%)
  Pallas kernels  27.5 us (7%)
  starting transfers between devices  26.6 us (7%)
  between operations  15.7 us (4%)
    psum x1, blocking collectives, body(): gain_sums = lax.psum(jnp.stack([gain_attn_grad, gain_ffn_grad]), ('m',) + F)  43.7 us
    dot_general x14, matrix products, dot(): lax.dot_general(left, right, (dims, ((), ())), preferred_element_type=F32)  42.3 us
    psum x1, waiting for transfers between devices, reduce(): return lax.psum(owned, 'm')  39.1 us
    reduce_scatter x2, waiting for transfers between devices, reduce(): lax.psum_scatter(grad.astype(BF), F, scatter_dimension=0, tiled=True)  32.2 us
    unnamed x7, waiting for transfers between devices  30.3 us
    unnamed x95, local copies, waits for them, and re-layouts  18.3 us
    ppermute x12, starting transfers between devices, spread(): slab = lax.ppermute(slab, 'm', [(i, i ^ k) for i in range(groups)])  17.5 us
    pallas_call x1, Pallas kernels, attend_back(): pl.pallas_call(kernel, grid=(pairs,), in_specs=[pl.BlockSpec((1, tokens),...  14.4 us
  transfers between devices with their start and end apart: 33, of which 10 were waited for; matrix products, arithmetic and copies ran while one was open for 24% of the time, Pallas kernels for 7%

profile of v1, /device:TPU:0, one launch (start us, length us, event | category | flops | bytes accessed | tf_op | source)
XLA Modules:
  0.0 387.2 jit_solution(16143156996031260108)
XLA Ops:
  10.9 2.9 collective-permute-start.4
  13.9 1.5 collective-permute-start.5
  16.4 1.6 collective-permute-start
  18.0 2.6 collective-permute-start.1
  20.8 2.3 reshape.163
  23.1 3.0 reshape.165
  28.8 1.9 fusion.21
  32.8 4.2 %collective-permute-done.1 = bf16[144,768]{1,0:T(8,128)(2,1)} collective-permute-done((bf16[144,768]{1,0:T(8,128)(2,1)}, bf16[144,768]{1,0:T(8,128)(2,1)}, u32[]{:S(2)}, u32[]{:S(2)}) %collective-permute-start.1) | collective-permute-done | bytes 221216 | tf_op jit(solution)/shard_map/ppermute | solution.py:236
  44.5 8.5 %collective-permute-done.6 = bf16[96,1536]{1,0:T(8,128)(2,1)S(1)} collective-permute-done((bf16[96,1536]{1,0:T(8,128)(2,1)S(1)}, bf16[96,1536]{1,0:T(8,128)(2,1)S(1)}, u32[]{:S(2)}, u32[]{:S(2)}) %collective-permute-start.6) | collective-permute-done | bytes 294944 | tf_op jit(solution)/shard_map/ppermute | solution.py:260
  55.6 13.1 %attend.1 = (bf16[1024,384]{1,0:T(8,128)(2,1)S(1)}, bf16[1024,384]{1,0:T(8,128)(2,1)S(1)}, bf16[1024,384]{1,0:T(8,128)(2,1)S(1)}, bf16[1024,384]{1,0:T(8,128)(2,1)S(1)}, f32[3,8,1024]{2,1,0:T(8,128)S(1)}) custom-call(f32[1,1024]{1,0:T(1,128)S(1)} %convert.4.refs_0_, bf16[1024,768]{1,0:T(8,128)(2,1)S(1)} %bitcast.161, ...), custom_call_target="tpu_custom_call" | custom-call | flops 3422552064 | bytes 8388608 | tf_op jit(solution)/shard_map/attend/pallas_call | solution.py:105
  68.9 3.2 fusion.29
  75.0 2.4 collective-permute-start.15
  78.8 8.4 %all-gather = bf16[4,192,2]{1,2,0:T(2,128)(2,1)S(1)} all-gather(bf16[1,192,2]{1,2,0:T(2,128)(2,1)S(1)} %maximum_bitcast_fusion), channel_id=1, replica_groups=mesh['m'=4,'r'=2,'y'=2,'x'=2] {'y','x'}, dimensions={0}, use_global_device_ids=true | all-gather | bytes 3840 | tf_op jit(solution)/shard_map/all_gather | solution.py:300
  89.4 4.6 %multiply_reduce_fusion.3 = (f32[1024]{0:T(1024)S(1)}, f32[1024,768]{1,0:T(8,128)}) fusion(f32[1024,768]{1,0:T(8,128)} %get-tuple-element.91, bf16[1024,768]{1,0:T(8,128)(2,1)} %collective-permute-done.9, bf16[4,2,128,768]{3,2,1,0:T(8,128)(2,1)S(1)} %fusion.8), kind=kLoop, calls=%fused_computation.22 | loop fusion | flops 4717568 | bytes 9441280 | tf_op jit(solution)/shard_map/reduce_sum | solution.py:215
  93.9 6.3 %fusion.24 = f32[1024,2048]{1,0:T(8,128)S(1)} fusion(bf16[768,2048]{1,0:T(8,128)(2,1)} %all-gather.4.cloned.1.call-done, f32[1024,768]{1,0:T(8,128)} %get-tuple-element.42, f32[768]{0:T(1024)S(1)} %get-tuple-element.32, f32[1024]{0:T(1024)S(1)} %add_rsqrt_fusion.1), kind=kOutput, calls=%fused_computation.139 | convolution fusion | flops 3223584768 | bytes 14687232 | tf_op jit(solution)/shard_map/dot_general | solution.py:19
  100.3 3.3 copy-done.23
  103.6 2.8 multiply_convert_fusion.2
  106.4 4.1 %all-gather.6.cloned.1.call-done = bf16[1024,768]{1,0:T(8,128)(2,1)} async-done(((bf16[256,768]{1,0:T(8,128)(2,1)}), bf16[1024,768]{1,0:T(8,128)(2,1)}) %all-gather.6.cloned.1.call-update) | async-done | bytes 1572880 | tf_op jit(solution)/shard_map/all_gather | solution.py:299
  110.5 3.8 fusion.30
  117.2 1.7 collective-permute-done.17
  120.4 1.7 copy-done.17
  124.4 2.0 fusion.4
  126.4 3.2 multiply_convert_fusion.1
  131.6 5.3 %convolution_convert_fusion = bf16[768,2048]{1,0:T(8,128)(2,1)} fusion(bf16[1024,1024]{1,0:T(8,128)(2,1)S(1)} %get-tuple-element.44, bf16[1024,1024]{1,0:T(8,128)(2,1)S(1)} %get-tuple-element.43, f32[1024,768]{1,0:T(8,128)S(1)} %copy-done.17, f32[768]{0:T(1024)S(1)} %get-tuple-element.32, f32[1024]{0:T(1024)S(1)} %add_rsqrt_fusion.1), kind=kOutput, calls=%fused_computation.10 | convolution fusion | flops 3233546240 | bytes 10492928 | tf_op jit(solution)/shard_map/dot_general | solution.py:19
  137.0 6.6 %fusion.31 = (bf16[1024,768]{1,0:T(8,128)(2,1)S(1)}, f32[1024,768]{1,0:T(8,128)S(1)}) fusion(bf16[768,2048]{1,0:T(8,128)(2,1)} %all-gather.4.cloned.1.call-done, bf16[1024,1024]{1,0:T(8,128)(2,1)} %copy-done.42, bf16[1024,1024]{1,0:T(8,128)(2,1)} %copy-done.41), kind=kOutput, calls=%fused_computation.146 | convolution fusion | flops 3230400512 | bytes 12058624 | tf_op jit(solution)/shard_map/dot_general | solution.py:19
  143.9 3.2 collective-permute-done.18
  148.1 2.4 fusion.25
  152.7 14.4 %attend_back.1 = (bf16[1024,384]{1,0:T(8,128)(2,1)S(1)}, bf16[1024,384]{1,0:T(8,128)(2,1)S(1)}, bf16[1024,384]{1,0:T(8,128)(2,1)S(1)}) custom-call(f32[1,1024]{1,0:T(1,128)S(1)} %convert.4.refs_0_, bf16[1024,768]{1,0:T(8,128)(2,1)} %copy-done.27, bf16[384,768]{1,0:T(8,128)(2,1)S(1)} %maximum_select_fusion.refs_2_, bf16[1024,384]{1,0:T(8,128)(2,1)S(1)} %copy-done.11, ...), custom_call_target="tpu_custom_call" | custom-call | flops 4630511616 | bytes 8388608 | tf_op jit(solution)/shard_map/attend_back/pallas_call | solution.py:189
  170.2 2.5 copy.94
  173.0 5.7 %convolution_convert_fusion.1 = bf16[1024,768]{1,0:T(8,128)(2,1)} fusion(bf16[1024,1024]{1,0:T(8,128)(2,1)} %multiply_convert_fusion.2, f32[1024,768]{1,0:T(8,128)} %copy-done.21), kind=kOutput, calls=%fused_computation.32 | convolution fusion | flops 1612185600 | bytes 6815744 | tf_op jit(solution)/shard_map/dot_general | solution.py:19
  181.1 2.4 collective-permute-start.12
  186.2 2.7 add_add_fusion
  188.9 2.2 copy.98
  191.1 30.2 %reduce-scatter.10.cloned.1.call-done = bf16[192,1536]{1,0:T(8,128)(2,1)} async-done(((bf16[768,1536]{1,0:T(8,128)(2,1)}), bf16[192,1536]{1,0:T(8,128)(2,1)}) %reduce-scatter.10.cloned.1.call-update) | async-done | bytes 589840
  221.3 2.2 copy.95
  223.6 32.2 %reduce-scatter.8.cloned.1.call-done = bf16[256,768]{1,0:T(8,128)(2,1)} async-done(((bf16[1024,768]{1,0:T(8,128)(2,1)}), bf16[256,768]{1,0:T(8,128)(2,1)}) %reduce-scatter.8.cloned.1.call-update) | async-done | bytes 393232 | tf_op jit(solution)/shard_map/reduce_scatter | solution.py:382
  255.7 1.5 fusion.12
  257.5 43.7 %psum.31 = f32[2,768]{1,0:T(2,128)S(1)} all-reduce(f32[2,768]{1,0:T(2,128)S(1)} %pad_maximum_fusion.10), channel_id=1, replica_groups=mesh['m'=4,'r'=2,'y'=2,'x'=2] {'m','y','x'}, use_global_device_ids=true, to_apply=%region_12.13 | all-reduce | flops 1536 | bytes 12288 | tf_op jit(solution)/shard_map/psum | solution.py:396
  301.2 2.2 fusion.10
  304.7 4.4 %collective-permute-start.22 = (bf16[128,768]{1,0:T(8,128)(2,1)}, bf16[128,768]{1,0:T(8,128)(2,1)}, u32[]{:S(2)}, u32[]{:S(2)}) collective-permute-start(bf16[128,768]{1,0:T(8,128)(2,1)} %get-tuple-element.75), channel_id=1, source_target_pairs={{0,24},{8,16},{16,8},{24,0},{1,25},{9,17},{17,9},{25,1},{2,26},{10... | collective-permute-start | bytes 589832 | tf_op jit(solution)/shard_map/ppermute | solution.py:236
  309.2 3.1 collective-permute-done.20
  312.2 39.1 %all-reduce.4.cloned.1.call-done = (bf16[192,1536]{0,1:T(8,128)(2,1)}, bf16[192,8,256]{2,1,0:T(8,128)(2,1)}, bf16[256,768]{1,0:T(8,128)(2,1)}) async-done(((bf16[192,1536]{0,1:T(8,128)(2,1)}, bf16[192,8,256]{2,1,0:T(8,128)(2,1)}, bf16[256,768]{1,0:T(8,128)(2,1)}), (bf16[192,1536]{0,1:T(8,128)(2,1)}, bf16[192,8,256]{2,1,0:T(8,128)(2,1)}, bf16[256,768]{1,0:T(8,128)(2,1)})) %all-reduce.4.cloned.1.call-update) | async-done | bytes 1769488 | tf_op jit(solution)/shard_map/psum | solution.py:383
  364.6 1.6 copy.86
  366.4 1.6 copy.87
  368.0 3.6 maximum_convert_fusion.1
  371.7 2.5 slice_bitcast_fusion
  374.2 3.4 reshape.171
  377.5 2.4 reshape.172
  (238 shorter events, 61.3 us)
Async XLA Ops:
  7.2 70.7 %copy-start = (bf16[512,768]{1,0:T(8,128)(2,1)S(1)}, bf16[512,768]{1,0:T(8,128)(2,1)}, u32[]{:S(2)}) copy-start(bf16[512,768]{1,0:T(8,128)(2,1)} %param.20) | copy-start | bytes 2359300
  7.2 8.2 %copy-start.37 = (s32[4,1,128]{2,1,0:T(1,128)S(1)}, s32[4,1,128]{2,1,0:T(1,128)}, u32[]{:S(2)}) copy-start(s32[4,1,128]{2,1,0:T(1,128)} %param.13) | copy-start | bytes 6148
  7.2 8.2 %copy-start.30 = (bf16[4,1,128,768]{3,2,1,0:T(8,128)(2,1)S(1)}, bf16[4,1,128,768]{3,2,1,0:T(8,128)(2,1)}, u32[]{:S(2)}) copy-start(bf16[4,1,128,768]{3,2,1,0:T(8,128)(2,1)} %param.12) | copy-start | bytes 2359300
  7.2 86.7 %all-gather.4.cloned.1.call-start = ((), (), s32[]{:S(2)}) async-start(), calls=%async_computation.3 | async-start | bytes 3932160 | tf_op jit(solution)/shard_map/all_gather | solution.py:298
  10.9 29.7 %collective-permute-start.4 = (bf16[192,1536]{1,0:T(8,128)(2,1)}, bf16[192,1536]{1,0:T(8,128)(2,1)}, u32[]{:S(2)}, u32[]{:S(2)}) collective-permute-start(bf16[192,1536]{1,0:T(8,128)(2,1)} %pad_maximum_fusion.7), channel_id=1, source_target_pairs={{0,1},{1,0},{2,3},{3,2},{4,5},{5,4},{6,7},{7,6},{8,9},{9,8},{10,11... | collective-permute-start | bytes 1769480 | tf_op jit(solution)/shard_map/ppermute | solution.py:258
  13.9 25.2 %collective-permute-start.5 = (bf16[192,1536]{1,0:T(8,128)(2,1)}, bf16[192,1536]{1,0:T(8,128)(2,1)}, u32[]{:S(2)}, u32[]{:S(2)}) collective-permute-start(bf16[192,1536]{1,0:T(8,128)(2,1)} %pad_maximum_fusion.7), channel_id=1, source_target_pairs={{0,2},{2,0},{1,3},{3,1},{4,6},{6,4},{5,7},{7,5},{8,10},{10,8},{9,1... | collective-permute-start | bytes 1769480 | tf_op jit(solution)/shard_map/ppermute | solution.py:259
  16.4 15.4 %collective-permute-start = (bf16[144,768]{1,0:T(8,128)(2,1)}, bf16[144,768]{1,0:T(8,128)(2,1)}, u32[]{:S(2)}, u32[]{:S(2)}) collective-permute-start(bf16[144,768]{1,0:T(8,128)(2,1)} %get-tuple-element.71), channel_id=1, source_target_pairs={{0,8},{8,0},{16,24},{24,16},{1,9},{9,1},{17,25},{25,17},{2,10},{10... | collective-permute-start | bytes 663560 | tf_op jit(solution)/shard_map/ppermute | solution.py:236
  18.0 19.1 %collective-permute-start.1 = (bf16[144,768]{1,0:T(8,128)(2,1)}, bf16[144,768]{1,0:T(8,128)(2,1)}, u32[]{:S(2)}, u32[]{:S(2)}) collective-permute-start(bf16[144,768]{1,0:T(8,128)(2,1)} %get-tuple-element.70), channel_id=1, source_target_pairs={{0,16},{8,24},{16,0},{24,8},{1,17},{9,25},{17,1},{25,9},{2,18},{10... | collective-permute-start | bytes 663560 | tf_op jit(solution)/shard_map/ppermute | solution.py:236
  20.6 17.4 %collective-permute-start.2 = (bf16[144,768]{1,0:T(8,128)(2,1)}, bf16[144,768]{1,0:T(8,128)(2,1)}, u32[]{:S(2)}, u32[]{:S(2)}) collective-permute-start(bf16[144,768]{1,0:T(8,128)(2,1)} %get-tuple-element.69), channel_id=1, source_target_pairs={{0,24},{8,16},{16,8},{24,0},{1,25},{9,17},{17,9},{25,1},{2,26},{10... | collective-permute-start | bytes 663560 | tf_op jit(solution)/shard_map/ppermute | solution.py:236
  28.4 82.0 %all-gather.6.cloned.1.call-start = ((), (), s32[]{:S(2)}) async-start(), calls=%async_computation.4 | async-start | bytes 1966080 | tf_op jit(solution)/shard_map/all_gather | solution.py:299
  31.6 24.0 %copy-start.8 = (f32[1024,128]{1,0:T(8,128)}, f32[1024,128]{1,0:T(8,128)S(1)}, u32[]{:S(2)}) copy-start(f32[1024,128]{1,0:T(8,128)S(1)} %get-tuple-element.103.refs_4_.refs_9_) | copy-start | bytes 1572868
  39.0 16.3 %collective-permute-start.3 = (bf16[4,144,768]{2,1,0:T(8,128)(2,1)S(1)}, bf16[4,144,768]{2,1,0:T(8,128)(2,1)S(1)}, u32[]{:S(2)}, u32[]{:S(2)}) collective-permute-start(bf16[4,144,768]{2,1,0:T(8,128)(2,1)S(1)} %bitcast_dynamic-update-slice_fusion.5), channel_id=1, source_target_pairs={{0,4},{4,0},{1,5},{5,1},{2,6},{6,2},{3,7},{7,3},{8,12},{12,8},{9,1... | collective-permute-start | bytes 2654216 | tf_op jit(solution)/shard_map/ppermute | solution.py:242
  40.0 13.0 %collective-permute-start.6 = (bf16[96,1536]{1,0:T(8,128)(2,1)S(1)}, bf16[96,1536]{1,0:T(8,128)(2,1)S(1)}, u32[]{:S(2)}, u32[]{:S(2)}) collective-permute-start(bf16[96,1536]{1,0:T(8,128)(2,1)S(1)} %slice.82), channel_id=1, source_target_pairs={{0,1},{1,0},{2,3},{3,2},{4,5},{5,4},{6,7},{7,6},{8,9},{9,8},{10,11... | collective-permute-start | bytes 884744 | tf_op jit(solution)/shard_map/ppermute | solution.py:260
  41.7 11.8 %collective-permute-start.7 = (bf16[96,1536]{1,0:T(8,128)(2,1)S(1)}, bf16[96,1536]{1,0:T(8,128)(2,1)S(1)}, u32[]{:S(2)}, u32[]{:S(2)}) collective-permute-start(bf16[96,1536]{1,0:T(8,128)(2,1)S(1)} %slice.83), channel_id=1, source_target_pairs={{0,2},{2,0},{1,3},{3,1},{4,6},{6,4},{5,7},{7,5},{8,10},{10,8},{9,1... | collective-permute-start | bytes 884744 | tf_op jit(solution)/shard_map/ppermute | solution.py:261
  54.9 13.8 %collective-permute-start.8 = (bf16[384,384]{1,0:T(8,128)(2,1)S(1)}, bf16[384,384]{1,0:T(8,128)(2,1)S(1)}, u32[]{:S(2)}, u32[]{:S(2)}) collective-permute-start(bf16[384,384]{1,0:T(8,128)(2,1)S(1)} %get-tuple-element.84), channel_id=1, source_target_pairs={{0,4},{4,0},{1,5},{5,1},{2,6},{6,2},{3,7},{7,3},{8,12},{12,8},{9,1... | collective-permute-start | bytes 884744 | tf_op jit(solution)/shard_map/ppermute | solution.py:314
  72.1 6.6 %copy-start.39 = (bf16[192]{0:T(256)(128)(2,1)S(1)}, bf16[192]{0:T(256)(128)(2,1)}, u32[]{:S(2)}) copy-start(bf16[192]{0:T(256)(128)(2,1)} %param.21) | copy-start | bytes 1156
  72.1 6.6 %copy-start.40 = (bf16[192]{0:T(256)(128)(2,1)S(1)}, bf16[192]{0:T(256)(128)(2,1)}, u32[]{:S(2)}) copy-start(bf16[192]{0:T(256)(128)(2,1)} %param.22) | copy-start | bytes 1156
  72.1 17.2 %collective-permute-start.9 = (bf16[1024,768]{1,0:T(8,128)(2,1)}, bf16[1024,768]{1,0:T(8,128)(2,1)}, u32[]{:S(2)}, u32[]{:S(2)}) collective-permute-start(bf16[1024,768]{1,0:T(8,128)(2,1)} %get-tuple-element.90), channel_id=1, source_target_pairs={{0,4},{4,0},{1,5},{5,1},{2,6},{6,2},{3,7},{7,3},{8,12},{12,8},{9,1... | collective-permute-start | bytes 4718600 | tf_op jit(solution)/shard_map/ppermute | solution.py:250
  73.5 14.9 %collective-permute-start.14 = (bf16[128,768]{1,0:T(8,128)(2,1)}, bf16[128,768]{1,0:T(8,128)(2,1)}, u32[]{:S(2)}, u32[]{:S(2)}) collective-permute-start(bf16[128,768]{1,0:T(8,128)(2,1)} %get-tuple-element.79), channel_id=1, source_target_pairs={{0,8},{8,0},{16,24},{24,16},{1,9},{9,1},{17,25},{25,17},{2,10},{10... | collective-permute-start | bytes 589832 | tf_op jit(solution)/shard_map/ppermute | solution.py:236
  75.0 39.4 %collective-permute-start.15 = (bf16[128,768]{1,0:T(8,128)(2,1)}, bf16[128,768]{1,0:T(8,128)(2,1)}, u32[]{:S(2)}, u32[]{:S(2)}) collective-permute-start(bf16[128,768]{1,0:T(8,128)(2,1)} %get-tuple-element.80), channel_id=1, source_target_pairs={{0,16},{8,24},{16,0},{24,8},{1,17},{9,25},{17,1},{25,9},{2,18},{10... | collective-permute-start | bytes 589832 | tf_op jit(solution)/shard_map/ppermute | solution.py:236
  77.4 38.0 %collective-permute-start.16 = (bf16[128,768]{1,0:T(8,128)(2,1)}, bf16[128,768]{1,0:T(8,128)(2,1)}, u32[]{:S(2)}, u32[]{:S(2)}) collective-permute-start(bf16[128,768]{1,0:T(8,128)(2,1)} %get-tuple-element.78), channel_id=1, source_target_pairs={{0,24},{8,16},{16,8},{24,0},{1,25},{9,17},{17,9},{25,1},{2,26},{10... | collective-permute-start | bytes 589832 | tf_op jit(solution)/shard_map/ppermute | solution.py:236
  78.7 110.2 %reduce-scatter.6.cloned.1.call-start = ((), (), s32[]{:S(2)}) async-start(), calls=%async_computation.5 | async-start | bytes 3932160 | tf_op jit(solution)/shard_map/reduce_scatter | solution.py:382
  114.3 6.1 %collective-permute-start.10 = (bf16[1024,768]{1,0:T(8,128)(2,1)S(1)}, bf16[1024,768]{1,0:T(8,128)(2,1)S(1)}, u32[]{:S(2)}, u32[]{:S(2)}) collective-permute-start(bf16[1024,768]{1,0:T(8,128)(2,1)S(1)} %get-tuple-element.92), channel_id=1, source_target_pairs={{0,4},{4,0},{1,5},{5,1},{2,6},{6,2},{3,7},{7,3},{8,12},{12,8},{9,1... | collective-permute-start | bytes 4718600 | tf_op jit(solution)/shard_map/ppermute | solution.py:250
  116.3 2.6 collective-permute-start.17
  122.1 4.2 %slice-start = ((s8[8388608]{0:T(1024)(128)(4,1)}), s8[4194304]{0:T(1024)(128)(4,1)S(1)}, s32[]{:S(2)}) async-start(s8[8388608]{0:T(1024)(128)(4,1)} %bitcast.171), calls=%async_computation.9 | async-start | bytes 8388608
  136.9 84.4 %reduce-scatter.10.cloned.1.call-start = ((), (), s32[]{:S(2)}) async-start(), calls=%async_computation.7 | async-start | bytes 2949120
  137.0 10.1 %copy-start.18 = (f32[1024,768]{1,0:T(8,128)S(1)}, f32[1024,768]{1,0:T(8,128)}, u32[]{:S(2)}) copy-start(f32[1024,768]{1,0:T(8,128)} %get-tuple-element.42) | copy-start | bytes 9437188
  137.0 10.1 %copy-start.22 = (f32[1024,768]{1,0:T(8,128)S(1)}, f32[1024,768]{1,0:T(8,128)}, u32[]{:S(2)}) copy-start(f32[1024,768]{1,0:T(8,128)} %copy-done.21) | copy-start | bytes 9437188
  143.6 3.5 collective-permute-start.18
  151.7 18.2 %collective-permute-start.23 = (bf16[384,384]{0,1:T(8,128)(2,1)S(1)}, bf16[384,384]{0,1:T(8,128)(2,1)S(1)}, u32[]{:S(2)}, u32[]{:S(2)}) collective-permute-start(bf16[384,384]{0,1:T(8,128)(2,1)S(1)} %get-tuple-element.82), channel_id=1, source_target_pairs={{0,4},{4,0},{1,5},{5,1},{2,6},{6,2},{3,7},{7,3},{8,12},{12,8},{9,1... | collective-permute-start | bytes 884744 | tf_op jit(solution)/shard_map/ppermute | solution.py:373
  172.7 83.0 %reduce-scatter.8.cloned.1.call-start = ((), (), s32[]{:S(2)}) async-start(), calls=%async_computation.6 | async-start | bytes 1966080 | tf_op jit(solution)/shard_map/reduce_scatter | solution.py:382
  173.0 5.9 %copy-start.24 = (bf16[1024,768]{1,0:T(8,128)(2,1)S(1)}, bf16[1024,768]{1,0:T(8,128)(2,1)}, u32[]{:S(2)}) copy-start(bf16[1024,768]{1,0:T(8,128)(2,1)} %get-tuple-element.46) | copy-start | bytes 4718596
  178.7 5.3 %copy-start.5 = (bf16[1024,384]{1,0:T(8,128)(2,1)S(1)}, bf16[1024,384]{1,0:T(8,128)(2,1)}, u32[]{:S(2)}) copy-start(bf16[1024,384]{1,0:T(8,128)(2,1)} %copy-done.4) | copy-start | bytes 2359300
  178.7 172.6 %all-reduce.4.cloned.1.call-start = ((), (), s32[]{:S(2)}) async-start(), calls=%async_computation.8 | async-start | bytes 3932160 | tf_op jit(solution)/shard_map/psum | solution.py:383
  178.8 5.2 %copy-start.20 = (bf16[4,192,1536]{2,1,0:T(8,128)(2,1)S(1)}, bf16[4,192,1536]{2,1,0:T(8,128)(2,1)}, u32[]{:S(2)}) copy-start(bf16[4,192,1536]{2,1,0:T(8,128)(2,1)} %copy-done.19) | copy-start | bytes 7077892
  179.7 77.7 %collective-permute-start.11 = (bf16[128,768]{1,0:T(8,128)(2,1)}, bf16[128,768]{1,0:T(8,128)(2,1)S(1)}, u32[]{:S(2)}, u32[]{:S(2)}) collective-permute-start(bf16[128,768]{1,0:T(8,128)(2,1)} %get-tuple-element.67), channel_id=1, source_target_pairs={{0,8},{8,0},{16,24},{24,16},{1,9},{9,1},{17,25},{25,17},{2,10},{10... | collective-permute-start | bytes 589832 | tf_op jit(solution)/shard_map/ppermute | solution.py:236
  181.1 76.2 %collective-permute-start.12 = (bf16[128,768]{1,0:T(8,128)(2,1)S(1)}, bf16[128,768]{1,0:T(8,128)(2,1)S(1)}, u32[]{:S(2)}, u32[]{:S(2)}) collective-permute-start(bf16[128,768]{1,0:T(8,128)(2,1)S(1)} %get-tuple-element.66), channel_id=1, source_target_pairs={{0,16},{8,24},{16,0},{24,8},{1,17},{9,25},{17,1},{25,9},{2,18},{10... | collective-permute-start | bytes 589832 | tf_op jit(solution)/shard_map/ppermute | solution.py:236
  183.6 73.9 %collective-permute-start.13 = (bf16[128,768]{1,0:T(8,128)(2,1)S(1)}, bf16[128,768]{1,0:T(8,128)(2,1)S(1)}, u32[]{:S(2)}, u32[]{:S(2)}) collective-permute-start(bf16[128,768]{1,0:T(8,128)(2,1)S(1)} %get-tuple-element.65), channel_id=1, source_target_pairs={{0,24},{8,16},{16,8},{24,0},{1,25},{9,17},{17,9},{25,1},{2,26},{10... | collective-permute-start | bytes 589832 | tf_op jit(solution)/shard_map/ppermute | solution.py:236
  191.1 66.2 %copy-start.33 = (bf16[4,1,128,768]{3,2,1,0:T(8,128)(2,1)S(1)}, bf16[4,1,128,768]{3,2,1,0:T(8,128)(2,1)}, u32[]{:S(2)}) copy-start(bf16[4,1,128,768]{3,2,1,0:T(8,128)(2,1)} %copy-done.32) | copy-start | bytes 2359300
  257.2 43.9 %collective-permute-start.19 = (bf16[4,128,768]{2,1,0:T(8,128)(2,1)S(1)}, bf16[4,128,768]{2,1,0:T(8,128)(2,1)S(1)}, u32[]{:S(2)}, u32[]{:S(2)}) collective-permute-start(bf16[4,128,768]{2,1,0:T(8,128)(2,1)S(1)} %fusion.12), channel_id=1, source_target_pairs={{0,4},{4,0},{1,5},{5,1},{2,6},{6,2},{3,7},{7,3},{8,12},{12,8},{9,1... | collective-permute-start | bytes 2359304 | tf_op jit(solution)/shard_map/ppermute | solution.py:364
  257.4 100.3 %copy-start.34 = (bf16[4,1,128,768]{3,2,1,0:T(8,128)(2,1)}, bf16[4,1,128,768]{3,2,1,0:T(8,128)(2,1)S(1)}, u32[]{:S(2)}) copy-start(bf16[4,1,128,768]{3,2,1,0:T(8,128)(2,1)S(1)} %bitcast_dynamic-update-slice_fusion.16) | copy-start | bytes 2359300
  304.0 8.2 %collective-permute-start.20 = (bf16[128,768]{1,0:T(8,128)(2,1)S(1)}, bf16[128,768]{1,0:T(8,128)(2,1)S(1)}, u32[]{:S(2)}, u32[]{:S(2)}) collective-permute-start(bf16[128,768]{1,0:T(8,128)(2,1)S(1)} %get-tuple-element.77), channel_id=1, source_target_pairs={{0,8},{8,0},{16,24},{24,16},{1,9},{9,1},{17,25},{25,17},{2,10},{10... | collective-permute-start | bytes 589832 | tf_op jit(solution)/shard_map/ppermute | solution.py:236
  304.7 46.8 %collective-permute-start.21 = (bf16[128,768]{1,0:T(8,128)(2,1)S(1)}, bf16[128,768]{1,0:T(8,128)(2,1)S(1)}, u32[]{:S(2)}, u32[]{:S(2)}) collective-permute-start(bf16[128,768]{1,0:T(8,128)(2,1)S(1)} %get-tuple-element.76), channel_id=1, source_target_pairs={{0,16},{8,24},{16,0},{24,8},{1,17},{9,25},{17,1},{25,9},{2,18},{10... | collective-permute-start | bytes 589832 | tf_op jit(solution)/shard_map/ppermute | solution.py:236
  304.7 48.7 %collective-permute-start.22 = (bf16[128,768]{1,0:T(8,128)(2,1)}, bf16[128,768]{1,0:T(8,128)(2,1)}, u32[]{:S(2)}, u32[]{:S(2)}) collective-permute-start(bf16[128,768]{1,0:T(8,128)(2,1)} %get-tuple-element.75), channel_id=1, source_target_pairs={{0,24},{8,16},{16,8},{24,0},{1,25},{9,17},{17,9},{25,1},{2,26},{10... | collective-permute-start | bytes 589832 | tf_op jit(solution)/shard_map/ppermute | solution.py:236
  351.4 3.9 %collective-permute-start.26 = (bf16[256,768]{1,0:T(8,128)(2,1)}, bf16[256,768]{1,0:T(8,128)(2,1)}, u32[]{:S(2)}, u32[]{:S(2)}) collective-permute-start(bf16[256,768]{1,0:T(8,128)(2,1)} %get-tuple-element.35), channel_id=1, source_target_pairs={{0,4},{4,0},{1,5},{5,1},{2,6},{6,2},{3,7},{7,3},{8,12},{12,8},{9,1... | collective-permute-start | bytes 1179656 | tf_op jit(solution)/shard_map/ppermute | solution.py:242
  352.9 4.9 %collective-permute-start.24 = (bf16[192,1536]{1,0:T(8,128)(2,1)S(1)}, bf16[192,1536]{1,0:T(8,128)(2,1)S(1)}, u32[]{:S(2)}, u32[]{:S(2)}) collective-permute-start(bf16[192,1536]{1,0:T(8,128)(2,1)S(1)} %copy.79), channel_id=1, source_target_pairs={{0,4},{4,0},{1,5},{5,1},{2,6},{6,2},{3,7},{7,3},{8,12},{12,8},{9,1... | collective-permute-start | bytes 1769480 | tf_op jit(solution)/shard_map/ppermute | solution.py:242
  355.2 7.9 %collective-permute-start.25 = (bf16[192,8,256]{2,1,0:T(8,128)(2,1)}, bf16[192,8,256]{2,1,0:T(8,128)(2,1)}, u32[]{:S(2)}, u32[]{:S(2)}) collective-permute-start(bf16[192,8,256]{2,1,0:T(8,128)(2,1)} %get-tuple-element.34), channel_id=1, source_target_pairs={{0,4},{4,0},{1,5},{5,1},{2,6},{6,2},{3,7},{7,3},{8,12},{12,8},{9,1... | collective-permute-start | bytes 2359304 | tf_op jit(solution)/shard_map/ppermute | solution.py:242
  374.2 5.8 %copy-start.1 = (bf16[512,768]{1,0:T(8,128)(2,1)S(1)}, bf16[512,768]{1,0:T(8,128)(2,1)}, u32[]{:S(2)}) copy-start(bf16[512,768]{1,0:T(8,128)(2,1)} %param.20) | copy-start | bytes 2359300
  (30 other events, 65.9 us)
Sparse Core Ops, SparseCore 0:
  28.6 48.4 all-gather.3
  79.5 30.9 all-gather.5
  137.0 43.9 reduce-scatter.5
  183.9 37.3 reduce-scatter.9
  224.7 30.9 reduce-scatter.7
  259.3 92.0 all-reduce.3
